TPU v7x, 512 devices: a whole 4x8x8 slice. The times are simulated.
512 devices in a mesh: dp: 16 (over z, core), ctx: 8 (over x, y_lo), mp: 4 (over y_hi).
Axes of the slice: x: 4, y: 8 (y_hi: 4, y_lo: 2; y = y_hi * 2 + y_lo), z: 8, core: 2. Of those that a mesh axis runs over, the one named last changes fastest.
Arguments:
- queries: bfloat16 [16, 1024, 4096], P('dp', 'ctx', 'mp'), may hold values from -1.6953125 to 1.6953125
- keys: bfloat16 [16, 1024, 4096], P('dp', 'ctx', 'mp'), may hold values from -1.6953125 to 1.6953125
- values: bfloat16 [16, 1024, 4096], P('dp', 'ctx', 'mp'), may hold values from -6 to 6
- cross_queries: bfloat16 [16, 1024, 4096], P('dp', 'ctx', 'mp'), may hold values from -1.6953125 to 1.6953125
- encoded_bank: bfloat16 [16, 64, 64, 896], P('dp', 'ctx'), may hold values from -6 to 6
- key_weight: bfloat16 [896, 4096], P(('dp', 'ctx'), 'mp'), may hold values from -0.1875 to 0.1875
- value_weight: bfloat16 [896, 4096], P(('dp', 'ctx'), 'mp'), may hold values from -0.1875 to 0.1875
- owner_ids: int32 [16, 16, 2], P('dp', 'ctx'), may hold values from 0 to 15, as said below
- unit_ids: int32 [16, 16, 2], P('dp', 'ctx'), may hold values from 0 to 6
- lengths: int32 [16], P('dp'), may hold values from 64 to 1024
Outputs:
- self_core: bfloat16 [16, 1024, 4096], P('dp', 'ctx', 'mp')
- cross_core: bfloat16 [16, 1024, 4096], P('dp', 'ctx', 'mp')
Inputs may be any that keep to these rules, and one draw needn't show every extreme that they name: `owner_ids`: among the 4 neighbours of the spans of one device (aligned blocks of 2 spans), no owner is named more than once.
All inputs are finite; a program needn't handle non-finite values.
Results may differ from a plain program's by a relative error of at most 0.006.
Values may be sent and summed in bfloat16 or wider, within the bound.
No kernel may reach another device: no remote copies, remote signals or barrier semaphores. Data moves between devices by JAX's collectives and lax.ppermute only.
A program may use at most 64 MiB of HBM per device.

v0:
```python
import math

import jax
import jax.numpy as jnp
from jax import lax
from jax.experimental import pallas as pl
from jax.experimental.pallas import tpu as pltpu
from jax.sharding import Mesh, PartitionSpec as P


HD = 128
SPAN = 64
NBR = 2
SCALE = 1.0 / math.sqrt(HD)
BF = jnp.bfloat16
F32 = jnp.float32
NT = (((1,), (1,)), ((), ()))


def pack_body(q_ref, k_ref, v_ref, o_ref):
    for h in range(o_ref.shape[0]):
        cols = slice(h * HD, (h + 1) * HD)
        o_ref[h, 0] = q_ref[0, :, cols]
        o_ref[h, 1] = k_ref[0, :, cols]
        o_ref[h, 2] = v_ref[0, :, cols]


def pack_heads(q, k, v):
    rows, width = q.shape[1:]
    return pl.pallas_call(
        pack_body,
        out_shape=jax.ShapeDtypeStruct((width // HD, 3, rows, HD), q.dtype),
        name="pack_heads",
    )(q, k, v)


def self_body(len_ref, x_ref, o_ref, k_ref, v_ref):
    blocks, _, rows, _ = x_ref.shape
    for j in range(blocks):
        k_ref[pl.ds(j * rows, rows), :] = x_ref[j, 1]
        v_ref[pl.ds(j * rows, rows), :] = x_ref[j, 2]
    length = len_ref[0]
    for i in range(blocks):
        width = (i + 1) * rows
        scores = lax.dot_general(
            x_ref[i, 0], k_ref[:width, :], NT, preferred_element_type=F32
        ) * SCALE
        row = lax.broadcasted_iota(jnp.int32, (rows, width), 0) + i * rows
        col = lax.broadcasted_iota(jnp.int32, (rows, width), 1)
        weights = jnp.where(col <= row, jnp.exp(scores), 0.0)
        sums = jnp.dot(weights.astype(BF), v_ref[:width, :], preferred_element_type=F32)
        result = sums / jnp.sum(weights, axis=1, keepdims=True)
        place = lax.broadcasted_iota(jnp.int32, (rows, HD), 0) + i * rows
        o_ref[i] = jnp.where(place < length, result, 0.0).astype(BF)


def self_attention(lengths, x):
    blocks, _, rows, _ = x.shape
    return pl.pallas_call(
        self_body,
        out_shape=jax.ShapeDtypeStruct((blocks, rows, HD), BF),
        in_specs=[
            pl.BlockSpec(memory_space=pltpu.SMEM),
            pl.BlockSpec(memory_space=pltpu.VMEM),
        ],
        scratch_shapes=[pltpu.VMEM((blocks * rows, HD), BF)] * 2,
        name="self_attention",
    )(lengths, x)


def offer_body(ids_ref, where_ref, bank_ref, o_ref):
    peers, part = o_ref.shape[0], o_ref.shape[1]
    asks = ids_ref.shape[1] // 4
    me, piece, core = where_ref[0], where_ref[1], where_ref[2]
    for z in range(peers // 2):
        for side in range(2):
            unit = jnp.int32(0)
            for t in range(asks):
                at = side * 2 * asks + (t // NBR) * 2 * NBR + t % NBR
                unit = jnp.where(ids_ref[z, at] == me, ids_ref[z, at + NBR], unit)
            start = pl.multiple_of(unit * SPAN + piece * part, part)
            o_ref[2 * z + jnp.bitwise_xor(core, side)] = bank_ref[pl.ds(start, part), :]


def offer_rows(ids, where, bank, part):
    zs = ids.shape[0]
    return pl.pallas_call(
        offer_body,
        out_shape=jax.ShapeDtypeStruct((2 * zs, part, bank.shape[1]), bank.dtype),
        in_specs=[
            pl.BlockSpec(memory_space=pltpu.SMEM),
            pl.BlockSpec(memory_space=pltpu.SMEM),
            pl.BlockSpec(memory_space=pltpu.VMEM),
        ],
        name="offer_rows",
    )(ids, where, bank)


def choose_body(own_ref, x_ref, o_ref):
    part = x_ref.shape[1]
    for t in range(o_ref.shape[0] // part):
        o_ref[t * part : (t + 1) * part, :] = x_ref[own_ref[0, t // NBR, t % NBR]]


def choose_rows(owners, received):
    asks = owners.shape[1] * owners.shape[2]
    _, part, enc = received.shape
    return pl.pallas_call(
        choose_body,
        out_shape=jax.ShapeDtypeStruct((asks * part, enc), received.dtype),
        in_specs=[
            pl.BlockSpec(memory_space=pltpu.SMEM),
            pl.BlockSpec(memory_space=pltpu.VMEM),
        ],
        name="choose_rows",
    )(owners, received)


def stage_body(own_ref, other_ref, k_ref, v_ref, o_ref):
    copies, rows, width = o_ref.shape
    depth, half = k_ref.shape
    lane = lax.broadcasted_iota(jnp.int32, (1, HD), 1)
    spans, each = own_ref.shape[1:]
    last = jnp.zeros((1, HD), F32)
    for side, ref in enumerate((own_ref, other_ref)):
        for s in range(spans):
            for t in range(each):
                at = (side * spans + s) * each + t
                last = jnp.where(lane == at, ref[0, s, t].astype(F32), last)
    pad = jnp.zeros((rows - depth, HD), F32)
    row = lax.broadcasted_iota(jnp.int32, pad.shape, 0)
    tail = jnp.where(row == rows - depth - 1, last, pad)
    for c in range(width // HD):
        src, at = (k_ref, c * HD) if c * HD < half else (v_ref, c * HD - half)
        top = src[:, at : at + HD].astype(F32)
        end = tail if c == 0 else pad
        block = jnp.concatenate([top, end], axis=0).astype(BF)
        for n in range(copies):
            o_ref[n, :, c * HD : (c + 1) * HD] = block


def stage_weights(ids, other_ids, key_weight, value_weight, copies):
    depth, width = key_weight.shape
    rows = -(-(depth + 1) // 8) * 8
    smem, vmem = pl.BlockSpec(memory_space=pltpu.SMEM), pl.BlockSpec(memory_space=pltpu.VMEM)
    return pl.pallas_call(
        stage_body,
        out_shape=jax.ShapeDtypeStruct((copies, rows, 2 * width), BF),
        in_specs=[smem, smem, vmem, vmem],
        name="stage_weights",
    )(ids, other_ids, key_weight, value_weight)


def cross_body(pos_ref, *refs):
    piece_refs, far_refs = refs[0:3], refs[3:5]
    pick_ref, ka_ref, kb_ref, va_ref, vb_ref, q_ref, o_ref, rows_ref = refs[5:]
    spans = q_ref.shape[1] // SPAN
    total = rows_ref.shape[0]
    each = total // spans
    half = pick_ref.shape[2]

    @pl.when(pl.program_id(0) == 0)
    def _():
        for side in range(2):
            cols = slice(side * half, (side + 1) * half)
            for p, piece in enumerate(piece_refs):
                part = jnp.dot(piece[...], pick_ref[side], preferred_element_type=F32)
                rows = part.shape[0] // spans
                for s in range(spans):
                    at = s * each + p * rows
                    rows_ref[at : at + rows, cols] = part[s * rows : (s + 1) * rows].astype(BF)
            for s, piece in enumerate(far_refs):
                part = jnp.dot(piece[...], pick_ref[side], preferred_element_type=F32)
                rows_ref[(s + 1) * each - part.shape[0] : (s + 1) * each, cols] = part.astype(BF)

    def project(a_ref, b_ref):
        return jnp.dot(rows_ref[:, :half], a_ref[...], preferred_element_type=F32) + jnp.dot(
            rows_ref[:, half:], b_ref[...], preferred_element_type=F32
        )

    key_proj = project(ka_ref, kb_ref)
    value_proj = project(va_ref, vb_ref).astype(BF)
    start, length = pos_ref[0], pos_ref[1]
    for h in range(o_ref.shape[2] // HD):
        cols = slice(h * HD, (h + 1) * HD)
        keys = key_proj[:, cols]
        scale = lax.rsqrt(jnp.mean(keys * keys, axis=1, keepdims=True) + 1e-06)
        keys = (keys * scale).astype(BF)
        values = value_proj[:, cols]
        for s in range(spans):
            own = slice(s * each, (s + 1) * each)
            scores = lax.dot_general(
                q_ref[0, s * SPAN : (s + 1) * SPAN, cols],
                keys[own],
                NT,
                preferred_element_type=F32,
            ) * SCALE
            weights = jnp.exp(scores)
            sums = jnp.dot(weights.astype(BF), values[own], preferred_element_type=F32)
            result = sums / jnp.sum(weights, axis=1, keepdims=True)
            place = lax.broadcasted_iota(jnp.int32, (SPAN, HD), 0) + (start + s * SPAN)
            o_ref[0, s * SPAN : (s + 1) * SPAN, cols] = jnp.where(
                place < length, result, 0.0
            ).astype(BF)


def cross_attention(pos, pieces, far, pick, own_w, other_w, queries):
    total = sum(p.shape[0] for p in pieces) + sum(p.shape[0] for p in far)
    half, width = own_w.shape[0], own_w.shape[1] // 2
    wide = 2 * HD
    steps = width // wide
    rows = queries.shape[1]
    whole = lambda x: pl.BlockSpec(x.shape, lambda j: (0,) * x.ndim)
    key_block = pl.BlockSpec((half, wide), lambda j: (0, j))
    value_block = pl.BlockSpec((half, wide), lambda j: (0, j + steps))
    tokens = pl.BlockSpec((1, rows, wide), lambda j: (0, 0, j))
    return pl.pallas_call(
        cross_body,
        grid=(steps,),
        out_shape=jax.ShapeDtypeStruct(queries.shape, BF),
        in_specs=[
            pl.BlockSpec(memory_space=pltpu.SMEM),
            *[whole(x) for x in pieces],
            *[whole(x) for x in far],
            whole(pick),
            key_block,
            key_block,
            value_block,
            value_block,
            tokens,
        ],
        out_specs=tokens,
        scratch_shapes=[pltpu.VMEM((total, 2 * half), BF)],
        name="cross_attention",
    )(pos, *pieces, *far, pick, own_w, other_w, own_w, other_w, queries)


def shift(x, axis, by):
    n = lax.axis_size(axis)
    return lax.ppermute(x, axis, [(i, (i + by) % n) for i in range(n)])


def local(
    queries,
    keys,
    values,
    cross_queries,
    encoded_bank,
    key_weight,
    value_weight,
    owner_ids,
    unit_ids,
    lengths,
):
    dp = ("z", "core")
    ctx_axes = ("x", "yl")
    core, x_at, y_at = (lax.axis_index(a) for a in ("core", "x", "yl"))
    n_z, n_x, n_y, n_mp = (lax.axis_size(a) for a in ("z", "x", "yl", "mp"))
    rows, width = queries.shape[1:]
    enc = encoded_bank.shape[3]
    asks = owner_ids.shape[1] * NBR
    part = 2 * SPAN // n_mp

    ids = jnp.concatenate([owner_ids, unit_ids], axis=2)
    staged = stage_weights(ids, shift(ids, "core", 1), key_weight, value_weight, n_z)
    depth, pad = key_weight.shape[0], staged.shape[1]
    column = lax.all_to_all(staged, "z", 0, 0, tiled=True)
    asked = column[:, pad - 1, : 4 * asks].astype(jnp.int32)

    where = jnp.stack([lax.axis_index(dp), lax.axis_index("mp"), core]).astype(jnp.int32)
    offered = offer_rows(asked, where, encoded_bank.reshape(-1, enc), part)
    received = lax.all_to_all(offered, dp, 0, 0, tiled=True)
    mine = choose_rows(owner_ids, received)
    left = shift(mine, "mp", 1)
    right = shift(mine, "mp", -1)
    mid = mine.shape[0] // 2
    far_left = shift(left[:mid], "mp", 1)
    far_right = shift(right[mid:], "mp", -1)
    pieces, far = (mine, left, right), (far_left, far_right)

    column = column.reshape(n_z * pad, 2 * width)
    beside = shift(column, "yl", 1)
    column = jnp.concatenate([column, beside], axis=0)
    w_left = shift(column, "x", 1)
    w_right = shift(column, "x", -1)
    w_far = shift(w_left, "x", 1)
    own_w = jnp.concatenate([column, w_left, w_right, w_far], axis=0)
    other_w = shift(own_w, "core", 1)

    heads = pack_heads(queries, keys, values)
    packed = lax.all_to_all(heads, ctx_axes, 0, 0, tiled=True)
    head = self_attention(lengths, packed)
    back = lax.all_to_all(head, ctx_axes, 0, 0, tiled=True)
    self_core = jnp.transpose(back, (1, 0, 2)).reshape(1, rows, width)

    half = own_w.shape[0]
    block = n_y * n_z * pad
    j = jnp.arange(half, dtype=jnp.int32)
    ring = j // block
    ahead = jnp.where(ring == 1, n_x - 1, jnp.where(ring == 2, 1, jnp.where(ring == 3, 2, 0)))
    y = jnp.bitwise_xor(y_at, (j // (n_z * pad)) & 1)
    ctx = ((x_at + ahead) & (n_x - 1)) * n_y + y
    i, z = j & (pad - 1), (j // pad) & (n_z - 1)
    dp_at = z * 2 + jnp.stack([core, 1 - core])[:, None]
    source = (dp_at * (n_x * n_y) + ctx) * depth + i
    source = jnp.where(i < depth, source, -1)
    entry = lax.broadcasted_iota(jnp.int32, (2, enc, half), 1)
    pick = (source[:, None, :] == entry).astype(BF)

    pos = jnp.stack([(x_at * n_y + y_at) * rows, lengths[0]]).astype(jnp.int32)
    cross_core = cross_attention(pos, pieces, far, pick, own_w, other_w, cross_queries)
    return self_core, cross_core


def solution(mesh):
    n_dp, n_ctx, n_mp = (mesh.shape[a] for a in ("dp", "ctx", "mp"))
    devices = mesh.devices.reshape(n_dp // 2, 2, n_ctx // 2, 2, n_mp)
    fine = Mesh(devices, ("z", "core", "x", "yl", "mp"))
    dp, ctx = ("z", "core"), ("x", "yl")
    tokens = P(dp, ctx, "mp")
    weight = P(dp + ctx, "mp")
    in_specs = (
        tokens,
        tokens,
        tokens,
        tokens,
        P(dp, ctx, None, None),
        weight,
        weight,
        P(dp, ctx, None),
        P(dp, ctx, None),
        P(dp),
    )
    return jax.shard_map(
        local, mesh=fine, in_specs=in_specs, out_specs=(tokens, tokens), check_vma=False
    )
```

profile of v0, /device:TPU:26, one launch (start us, length us, event | category | flops | bytes accessed | tf_op | source)
XLA Modules:
  0.0 132.5 jit_solution(903854652396237215)
XLA Ops:
  0.6 0.8 pad_add_fusion.own_ref
  1.4 1.9 %collective-permute-start = (s32[1,2,4]{2,1,0:T(2,128)S(1)}, s32[1,2,4]{2,1,0:T(2,128)S(1)}, u32[]{:S(2)}, u32[]{:S(2)}) collective-permute-start(s32[1,2,4]{2,1,0:T(2,128)S(1)} %pad_add_fusion.own_ref), channel_id=1, source_target_pairs={{0,32},{32,0},{1,33},{33,1},{2,34},{34,2},{3,35},{35,3},{4,36},{36... | collective-permute-start | bytes 104 | tf_op jit(solution)/shard_map/ppermute | solution.py:240
  3.3 1.1 collective-permute-done.other_ref
  4.4 0.0 copy-done.6
  4.5 0.6 copy-done.7
  5.0 1.5 %stage_weights.1 = bf16[8,8,2048]{2,1,0:T(8,128)(2,1)} custom-call(s32[1,2,4]{2,1,0:T(2,128)} %copy-done.6, s32[1,2,4]{2,1,0:T(2,128)} %copy-done.7, bf16[7,1024]{1,0:T(8,128)(2,1)} %k_ref.3, bf16[7,1024]{1,0:T(8,128)(2,1)} %v_ref.3), custom_call_target="tpu_custom_call" | custom-call | tf_op jit(solution)/shard_map/stage_weights/pallas_call | solution.py:146
  6.5 10.3 %all-to-all-start.2 = ((bf16[8,8,2048]{2,1,0:T(8,128)(2,1)}), bf16[8,8,2048]{2,1,0:T(8,128)(2,1)S(1)}, u32[]{:S(2)}, u32[]{:S(2)}) async-start(bf16[8,8,2048]{2,1,0:T(8,128)(2,1)} %stage_weights.1), calls=%async_computation.2 | async-start | bytes 524288 | tf_op jit(solution)/shard_map/all_to_all | solution.py:267
  16.8 12.2 %all-to-all-done.2 = bf16[8,8,2048]{2,1,0:T(8,128)(2,1)S(1)} async-done(((bf16[8,8,2048]{2,1,0:T(8,128)(2,1)}), bf16[8,8,2048]{2,1,0:T(8,128)(2,1)S(1)}, u32[]{:S(2)}, u32[]{:S(2)}) %all-to-all-start.2) | async-done | bytes 262176 | tf_op jit(solution)/shard_map/all_to_all | solution.py:267
  29.0 2.3 %collective-permute-start.5 = (bf16[64,2048]{1,0:T(8,128)(2,1)S(1)}, bf16[64,2048]{1,0:T(8,128)(2,1)S(1)}, u32[]{:S(2)}, u32[]{:S(2)}) collective-permute-start(bf16[64,2048]{1,0:T(8,128)(2,1)S(1)} %bitcast.11), channel_id=1, source_target_pairs={{0,4},{4,0},{1,5},{5,1},{2,6},{6,2},{3,7},{7,3},{8,12},{12,8},{9,1... | collective-permute-start | bytes 786440 | tf_op jit(solution)/shard_map/ppermute | solution.py:240
  31.4 0.6 pad_add_fusion.2.where_ref
  32.0 0.6 slice_convert_fusion
  32.6 2.3 %offer_rows.1 = bf16[16,32,896]{2,1,0:T(8,128)(2,1)} custom-call(s32[8,16]{1,0:T(8,128)} %bitcast.16, s32[3]{0:T(128)} %pad_add_fusion.2.where_ref, bf16[512,896]{1,0:T(8,128)(2,1)} %bitcast.15), custom_call_target="tpu_custom_call" | custom-call | tf_op jit(solution)/shard_map/offer_rows/pallas_call | solution.py:87
  34.9 3.6 %all-to-all-start.3 = ((bf16[16,32,896]{2,1,0:T(8,128)(2,1)}), bf16[16,32,896]{2,1,0:T(8,128)(2,1)S(1)}, u32[]{:S(2)}, u32[]{:S(2)}) async-start(bf16[16,32,896]{2,1,0:T(8,128)(2,1)} %offer_rows.1), calls=%async_computation.3 | async-start | bytes 1835008 | tf_op jit(solution)/shard_map/all_to_all | solution.py:272
  38.6 0.0 collective-permute-done.5
  38.6 3.4 %collective-permute-start.6 = (bf16[128,2048]{1,0:T(8,128)(2,1)S(1)}, bf16[128,2048]{1,0:T(8,128)(2,1)S(1)}, u32[]{:S(2)}, u32[]{:S(2)}) collective-permute-start(bf16[128,2048]{1,0:T(8,128)(2,1)S(1)} %pad_maximum_fusion), channel_id=1, source_target_pairs={{0,8},{8,16},{16,24},{24,0},{1,9},{9,17},{17,25},{25,1},{2,10},{10... | collective-permute-start | bytes 1572872 | tf_op jit(solution)/shard_map/ppermute | solution.py:240
  42.0 2.4 %collective-permute-start.7 = (bf16[128,2048]{1,0:T(8,128)(2,1)S(1)}, bf16[128,2048]{1,0:T(8,128)(2,1)S(1)}, u32[]{:S(2)}, u32[]{:S(2)}) collective-permute-start(bf16[128,2048]{1,0:T(8,128)(2,1)S(1)} %pad_maximum_fusion), channel_id=1, source_target_pairs={{0,24},{8,0},{16,8},{24,16},{1,25},{9,1},{17,9},{25,17},{2,26},{10... | collective-permute-start | bytes 1572872 | tf_op jit(solution)/shard_map/ppermute | solution.py:240
  44.5 10.1 %collective-permute-done.6 = bf16[128,2048]{1,0:T(8,128)(2,1)S(1)} collective-permute-done((bf16[128,2048]{1,0:T(8,128)(2,1)S(1)}, bf16[128,2048]{1,0:T(8,128)(2,1)S(1)}, u32[]{:S(2)}, u32[]{:S(2)}) %collective-permute-start.6) | collective-permute-done | bytes 524320 | tf_op jit(solution)/shard_map/ppermute | solution.py:240
  54.6 3.4 %collective-permute-start.8 = (bf16[128,2048]{1,0:T(8,128)(2,1)S(1)}, bf16[128,2048]{1,0:T(8,128)(2,1)S(1)}, u32[]{:S(2)}, u32[]{:S(2)}) collective-permute-start(bf16[128,2048]{1,0:T(8,128)(2,1)S(1)} %collective-permute-done.6), channel_id=1, source_target_pairs={{0,8},{8,16},{16,24},{24,0},{1,9},{9,17},{17,25},{25,1},{2,10},{10... | collective-permute-start | bytes 1572872 | tf_op jit(solution)/shard_map/ppermute | solution.py:240
  58.1 0.0 collective-permute-done.7
  58.1 11.6 %collective-permute-done.8 = bf16[128,2048]{1,0:T(8,128)(2,1)S(1)} collective-permute-done((bf16[128,2048]{1,0:T(8,128)(2,1)S(1)}, bf16[128,2048]{1,0:T(8,128)(2,1)S(1)}, u32[]{:S(2)}, u32[]{:S(2)}) %collective-permute-start.8) | collective-permute-done | bytes 524320 | tf_op jit(solution)/shard_map/ppermute | solution.py:240
  69.8 1.9 %collective-permute-start.9 = (bf16[512,2048]{1,0:T(8,128)(2,1)S(1)}, bf16[512,2048]{1,0:T(8,128)(2,1)}, u32[]{:S(2)}, u32[]{:S(2)}) collective-permute-start(bf16[512,2048]{1,0:T(8,128)(2,1)S(1)} %constant_dynamic-update-slice_fusion.refs_6_.refs_8_), channel_id=1, source_target_pairs={{0,32},{32,0},{1,33},{33,1},{2,34},{34,2},{3,35},{35,3},{4,36},{36... | collective-permute-start | bytes 6291464 | tf_op jit(solution)/shard_map/ppermute | solution.py:240
  71.7 2.2 %pack_heads.1 = bf16[8,3,128,128]{3,2,1,0:T(8,128)(2,1)} custom-call(bf16[1,128,1024]{2,1,0:T(8,128)(2,1)} %q_ref.1, bf16[1,128,1024]{2,1,0:T(8,128)(2,1)} %k_ref.2, bf16[1,128,1024]{2,1,0:T(8,128)(2,1)} %v_ref.2), custom_call_target="tpu_custom_call" | custom-call | tf_op jit(solution)/shard_map/pack_heads/pallas_call | solution.py:30
  73.9 0.0 all-to-all-done.3.x_ref
  73.9 8.1 %all-to-all-start = ((bf16[8,3,128,128]{3,2,1,0:T(8,128)(2,1)}), bf16[8,3,128,128]{3,2,1,0:T(8,128)(2,1)}, u32[]{:S(2)}, u32[]{:S(2)}) async-start(bf16[8,3,128,128]{3,2,1,0:T(8,128)(2,1)} %pack_heads.1), calls=%async_computation | async-start | bytes 1572864 | tf_op jit(solution)/shard_map/all_to_all | solution.py:291
  82.0 1.9 %choose_rows.1.refs_0_ = bf16[128,896]{1,0:T(8,128)(2,1)} custom-call(s32[1,2,2]{2,1,0:T(2,128)} %own_ref.1, bf16[16,32,896]{2,1,0:T(8,128)(2,1)} %copy-done.1), custom_call_target="tpu_custom_call" | custom-call | tf_op jit(solution)/shard_map/choose_rows/pallas_call | solution.py:108
  84.0 4.8 %collective-permute-start.1 = (bf16[128,896]{1,0:T(8,128)(2,1)}, bf16[128,896]{1,0:T(8,128)(2,1)S(1)}, u32[]{:S(2)}, u32[]{:S(2)}) collective-permute-start(bf16[128,896]{1,0:T(8,128)(2,1)} %choose_rows.1.refs_0_), channel_id=1, source_target_pairs={{0,1},{1,2},{2,3},{3,0},{4,5},{5,6},{6,7},{7,4},{8,9},{9,10},{10,1... | collective-permute-start | bytes 688136 | tf_op jit(solution)/shard_map/ppermute | solution.py:240
  88.8 1.9 %collective-permute-start.2 = (bf16[128,896]{1,0:T(8,128)(2,1)}, bf16[128,896]{1,0:T(8,128)(2,1)S(1)}, u32[]{:S(2)}, u32[]{:S(2)}) collective-permute-start(bf16[128,896]{1,0:T(8,128)(2,1)} %choose_rows.1.refs_0_), channel_id=1, source_target_pairs={{0,3},{1,0},{2,1},{3,2},{4,7},{5,4},{6,5},{7,6},{8,11},{9,8},{10,9... | collective-permute-start | bytes 688136 | tf_op jit(solution)/shard_map/ppermute | solution.py:240
  90.7 0.1 pad_add_fusion.3
  91.5 6.4 %all-to-all-done.x_ref = bf16[8,3,128,128]{3,2,1,0:T(8,128)(2,1)} async-done(((bf16[8,3,128,128]{3,2,1,0:T(8,128)(2,1)}), bf16[8,3,128,128]{3,2,1,0:T(8,128)(2,1)}, u32[]{:S(2)}, u32[]{:S(2)}) %all-to-all-start) | async-done | bytes 786464 | tf_op jit(solution)/shard_map/all_to_all | solution.py:291
  97.8 3.4 %self_attention.1 = bf16[8,128,128]{2,1,0:T(8,128)(2,1)} custom-call(s32[1]{0:T(128)S(6)} %copy.18.len_ref, bf16[8,3,128,128]{3,2,1,0:T(8,128)(2,1)} %all-to-all-done.x_ref), custom_call_target="tpu_custom_call" | custom-call | tf_op jit(solution)/shard_map/self_attention/pallas_call | solution.py:59
  101.3 5.7 %all-to-all-start.1 = ((bf16[8,128,128]{2,1,0:T(8,128)(2,1)}), bf16[8,128,128]{2,1,0:T(8,128)(2,1)S(1)}, u32[]{:S(2)}, u32[]{:S(2)}) async-start(bf16[8,128,128]{2,1,0:T(8,128)(2,1)} %self_attention.1), calls=%async_computation.1 | async-start | bytes 524288 | tf_op jit(solution)/shard_map/all_to_all | solution.py:293
  107.0 0.1 add_select_fusion
  107.0 0.0 collective-permute-done.1.refs_1_
  107.1 4.8 %collective-permute-start.3 = (bf16[64,896]{1,0:T(8,128)(2,1)S(1)}, bf16[64,896]{1,0:T(8,128)(2,1)S(1)}, u32[]{:S(2)}, u32[]{:S(2)}) collective-permute-start(bf16[64,896]{1,0:T(8,128)(2,1)S(1)} %slice.13), channel_id=1, source_target_pairs={{0,1},{1,2},{2,3},{3,0},{4,5},{5,6},{6,7},{7,4},{8,9},{9,10},{10,1... | collective-permute-start | bytes 344072 | tf_op jit(solution)/shard_map/ppermute | solution.py:240
  111.9 0.0 collective-permute-done.2.refs_2_
  111.9 1.9 %collective-permute-start.4 = (bf16[64,896]{1,0:T(8,128)(2,1)S(1)}, bf16[64,896]{1,0:T(8,128)(2,1)S(1)}, u32[]{:S(2)}, u32[]{:S(2)}) collective-permute-start(bf16[64,896]{1,0:T(8,128)(2,1)S(1)} %slice.14), channel_id=1, source_target_pairs={{0,3},{1,0},{2,1},{3,2},{4,7},{5,4},{6,5},{7,6},{8,11},{9,8},{10,9... | collective-permute-start | bytes 344072 | tf_op jit(solution)/shard_map/ppermute | solution.py:240
  113.9 1.9 %fusion.refs_5_ = bf16[2,896,512]{2,1,0:T(8,128)(2,1)} fusion(s32[2,512]{1,0:T(2,128)S(1)} %add_select_fusion), kind=kLoop, calls=%fused_computation.1 | loop fusion | flops 1835008 | bytes 1839104 | tf_op jit(solution)/shard_map/convert_element_type | solution.py:308
  115.8 0.6 pad_add_fusion.1.pos_ref
  116.5 0.0 all-to-all-done.1
  116.5 0.2 copy.12
  116.7 0.9 copy.13
  117.5 0.0 collective-permute-done.3.refs_3_
  117.5 4.0 %collective-permute-done.4.refs_4_ = bf16[64,896]{1,0:T(8,128)(2,1)S(1)} collective-permute-done((bf16[64,896]{1,0:T(8,128)(2,1)S(1)}, bf16[64,896]{1,0:T(8,128)(2,1)S(1)}, u32[]{:S(2)}, u32[]{:S(2)}) %collective-permute-start.4) | collective-permute-done | bytes 114720 | tf_op jit(solution)/shard_map/ppermute | solution.py:240
  121.6 0.0 collective-permute-done.9.refs_7_.refs_9_
  121.6 0.0 copy-done.3
  121.6 0.0 copy-done.4
  121.6 0.6 copy-done.5
  122.2 10.4 %cross_attention.1 = bf16[1,128,1024]{2,1,0:T(8,128)(2,1)} custom-call(s32[2]{0:T(128)} %pad_add_fusion.1.pos_ref, bf16[128,896]{1,0:T(8,128)(2,1)} %choose_rows.1.refs_0_, bf16[128,896]{1,0:T(8,128)(2,1)} %copy-done.2, bf16[128,896]{1,0:T(8,128)(2,1)} %copy-done.3, bf16[64,896]{1,0:T(8,128)(2,1)} %copy-done.4, bf16[64,896]{1,0:T(8,128)(2,1)} %copy-done.5, ...), custom_call_target="tpu_custom_call" | custom-call | tf_op jit(solution)/shard_map/cross_attention/pallas_call | solution.py:217
  (22 shorter events, 0.2 us)
Async XLA Ops:
  1.4 3.0 %copy-start.6 = (s32[1,2,4]{2,1,0:T(2,128)}, s32[1,2,4]{2,1,0:T(2,128)S(1)}, u32[]{:S(2)}) copy-start(s32[1,2,4]{2,1,0:T(2,128)S(1)} %pad_add_fusion.own_ref) | copy-start | bytes 100
  1.4 3.0 %collective-permute-start = (s32[1,2,4]{2,1,0:T(2,128)S(1)}, s32[1,2,4]{2,1,0:T(2,128)S(1)}, u32[]{:S(2)}, u32[]{:S(2)}) collective-permute-start(s32[1,2,4]{2,1,0:T(2,128)S(1)} %pad_add_fusion.own_ref), channel_id=1, source_target_pairs={{0,32},{32,0},{1,33},{33,1},{2,34},{34,2},{3,35},{35,3},{4,36},{36... | collective-permute-start | bytes 104 | tf_op jit(solution)/shard_map/ppermute | solution.py:240
  4.4 0.6 copy-start.7
  6.5 22.5 %all-to-all-start.2 = ((bf16[8,8,2048]{2,1,0:T(8,128)(2,1)}), bf16[8,8,2048]{2,1,0:T(8,128)(2,1)S(1)}, u32[]{:S(2)}, u32[]{:S(2)}) async-start(bf16[8,8,2048]{2,1,0:T(8,128)(2,1)} %stage_weights.1), calls=%async_computation.2 | async-start | bytes 524288 | tf_op jit(solution)/shard_map/all_to_all | solution.py:267
  29.0 9.5 %collective-permute-start.5 = (bf16[64,2048]{1,0:T(8,128)(2,1)S(1)}, bf16[64,2048]{1,0:T(8,128)(2,1)S(1)}, u32[]{:S(2)}, u32[]{:S(2)}) collective-permute-start(bf16[64,2048]{1,0:T(8,128)(2,1)S(1)} %bitcast.11), channel_id=1, source_target_pairs={{0,4},{4,0},{1,5},{5,1},{2,6},{6,2},{3,7},{7,3},{8,12},{12,8},{9,1... | collective-permute-start | bytes 786440 | tf_op jit(solution)/shard_map/ppermute | solution.py:240
  34.9 39.0 %all-to-all-start.3 = ((bf16[16,32,896]{2,1,0:T(8,128)(2,1)}), bf16[16,32,896]{2,1,0:T(8,128)(2,1)S(1)}, u32[]{:S(2)}, u32[]{:S(2)}) async-start(bf16[16,32,896]{2,1,0:T(8,128)(2,1)} %offer_rows.1), calls=%async_computation.3 | async-start | bytes 1835008 | tf_op jit(solution)/shard_map/all_to_all | solution.py:272
  38.6 16.0 %collective-permute-start.6 = (bf16[128,2048]{1,0:T(8,128)(2,1)S(1)}, bf16[128,2048]{1,0:T(8,128)(2,1)S(1)}, u32[]{:S(2)}, u32[]{:S(2)}) collective-permute-start(bf16[128,2048]{1,0:T(8,128)(2,1)S(1)} %pad_maximum_fusion), channel_id=1, source_target_pairs={{0,8},{8,16},{16,24},{24,0},{1,9},{9,17},{17,25},{25,1},{2,10},{10... | collective-permute-start | bytes 1572872 | tf_op jit(solution)/shard_map/ppermute | solution.py:240
  42.0 16.1 %collective-permute-start.7 = (bf16[128,2048]{1,0:T(8,128)(2,1)S(1)}, bf16[128,2048]{1,0:T(8,128)(2,1)S(1)}, u32[]{:S(2)}, u32[]{:S(2)}) collective-permute-start(bf16[128,2048]{1,0:T(8,128)(2,1)S(1)} %pad_maximum_fusion), channel_id=1, source_target_pairs={{0,24},{8,0},{16,8},{24,16},{1,25},{9,1},{17,9},{25,17},{2,26},{10... | collective-permute-start | bytes 1572872 | tf_op jit(solution)/shard_map/ppermute | solution.py:240
  54.6 15.2 %collective-permute-start.8 = (bf16[128,2048]{1,0:T(8,128)(2,1)S(1)}, bf16[128,2048]{1,0:T(8,128)(2,1)S(1)}, u32[]{:S(2)}, u32[]{:S(2)}) collective-permute-start(bf16[128,2048]{1,0:T(8,128)(2,1)S(1)} %collective-permute-done.6), channel_id=1, source_target_pairs={{0,8},{8,16},{16,24},{24,0},{1,9},{9,17},{17,25},{25,1},{2,10},{10... | collective-permute-start | bytes 1572872 | tf_op jit(solution)/shard_map/ppermute | solution.py:240
  69.8 14.2 %copy-start = (bf16[512,2048]{1,0:T(8,128)(2,1)}, bf16[512,2048]{1,0:T(8,128)(2,1)S(1)}, u32[]{:S(2)}) copy-start(bf16[512,2048]{1,0:T(8,128)(2,1)S(1)} %constant_dynamic-update-slice_fusion.refs_6_.refs_8_) | copy-start | bytes 6291460
  69.8 51.7 %collective-permute-start.9 = (bf16[512,2048]{1,0:T(8,128)(2,1)S(1)}, bf16[512,2048]{1,0:T(8,128)(2,1)}, u32[]{:S(2)}, u32[]{:S(2)}) collective-permute-start(bf16[512,2048]{1,0:T(8,128)(2,1)S(1)} %constant_dynamic-update-slice_fusion.refs_6_.refs_8_), channel_id=1, source_target_pairs={{0,32},{32,0},{1,33},{33,1},{2,34},{34,2},{3,35},{35,3},{4,36},{36... | collective-permute-start | bytes 6291464 | tf_op jit(solution)/shard_map/ppermute | solution.py:240
  73.9 8.1 %copy-start.1 = (bf16[16,32,896]{2,1,0:T(8,128)(2,1)}, bf16[16,32,896]{2,1,0:T(8,128)(2,1)S(1)}, u32[]{:S(2)}) copy-start(bf16[16,32,896]{2,1,0:T(8,128)(2,1)S(1)} %all-to-all-done.3.x_ref) | copy-start | bytes 2752516
  73.9 23.9 %all-to-all-start = ((bf16[8,3,128,128]{3,2,1,0:T(8,128)(2,1)}), bf16[8,3,128,128]{3,2,1,0:T(8,128)(2,1)}, u32[]{:S(2)}, u32[]{:S(2)}) async-start(bf16[8,3,128,128]{3,2,1,0:T(8,128)(2,1)} %pack_heads.1), calls=%async_computation | async-start | bytes 1572864 | tf_op jit(solution)/shard_map/all_to_all | solution.py:291
  84.0 23.1 %collective-permute-start.1 = (bf16[128,896]{1,0:T(8,128)(2,1)}, bf16[128,896]{1,0:T(8,128)(2,1)S(1)}, u32[]{:S(2)}, u32[]{:S(2)}) collective-permute-start(bf16[128,896]{1,0:T(8,128)(2,1)} %choose_rows.1.refs_0_), channel_id=1, source_target_pairs={{0,1},{1,2},{2,3},{3,0},{4,5},{5,6},{6,7},{7,4},{8,9},{9,10},{10,1... | collective-permute-start | bytes 688136 | tf_op jit(solution)/shard_map/ppermute | solution.py:240
  88.8 23.1 %collective-permute-start.2 = (bf16[128,896]{1,0:T(8,128)(2,1)}, bf16[128,896]{1,0:T(8,128)(2,1)S(1)}, u32[]{:S(2)}, u32[]{:S(2)}) collective-permute-start(bf16[128,896]{1,0:T(8,128)(2,1)} %choose_rows.1.refs_0_), channel_id=1, source_target_pairs={{0,3},{1,0},{2,1},{3,2},{4,7},{5,4},{6,5},{7,6},{8,11},{9,8},{10,9... | collective-permute-start | bytes 688136 | tf_op jit(solution)/shard_map/ppermute | solution.py:240
  101.3 15.2 %all-to-all-start.1 = ((bf16[8,128,128]{2,1,0:T(8,128)(2,1)}), bf16[8,128,128]{2,1,0:T(8,128)(2,1)S(1)}, u32[]{:S(2)}, u32[]{:S(2)}) async-start(bf16[8,128,128]{2,1,0:T(8,128)(2,1)} %self_attention.1), calls=%async_computation.1 | async-start | bytes 524288 | tf_op jit(solution)/shard_map/all_to_all | solution.py:293
  107.1 14.5 %copy-start.2 = (bf16[128,896]{1,0:T(8,128)(2,1)}, bf16[128,896]{1,0:T(8,128)(2,1)S(1)}, u32[]{:S(2)}) copy-start(bf16[128,896]{1,0:T(8,128)(2,1)S(1)} %collective-permute-done.1.refs_1_) | copy-start | bytes 688132
  107.1 10.4 %collective-permute-start.3 = (bf16[64,896]{1,0:T(8,128)(2,1)S(1)}, bf16[64,896]{1,0:T(8,128)(2,1)S(1)}, u32[]{:S(2)}, u32[]{:S(2)}) collective-permute-start(bf16[64,896]{1,0:T(8,128)(2,1)S(1)} %slice.13), channel_id=1, source_target_pairs={{0,1},{1,2},{2,3},{3,0},{4,5},{5,6},{6,7},{7,4},{8,9},{9,10},{10,1... | collective-permute-start | bytes 344072 | tf_op jit(solution)/shard_map/ppermute | solution.py:240
  111.9 9.6 %copy-start.3 = (bf16[128,896]{1,0:T(8,128)(2,1)}, bf16[128,896]{1,0:T(8,128)(2,1)S(1)}, u32[]{:S(2)}) copy-start(bf16[128,896]{1,0:T(8,128)(2,1)S(1)} %collective-permute-done.2.refs_2_) | copy-start | bytes 688132
  111.9 9.6 %collective-permute-start.4 = (bf16[64,896]{1,0:T(8,128)(2,1)S(1)}, bf16[64,896]{1,0:T(8,128)(2,1)S(1)}, u32[]{:S(2)}, u32[]{:S(2)}) collective-permute-start(bf16[64,896]{1,0:T(8,128)(2,1)S(1)} %slice.14), channel_id=1, source_target_pairs={{0,3},{1,0},{2,1},{3,2},{4,7},{5,4},{6,5},{7,6},{8,11},{9,8},{10,9... | collective-permute-start | bytes 344072 | tf_op jit(solution)/shard_map/ppermute | solution.py:240
  117.5 4.1 %copy-start.4 = (bf16[64,896]{1,0:T(8,128)(2,1)}, bf16[64,896]{1,0:T(8,128)(2,1)S(1)}, u32[]{:S(2)}) copy-start(bf16[64,896]{1,0:T(8,128)(2,1)S(1)} %collective-permute-done.3.refs_3_) | copy-start | bytes 344068
  121.5 0.6 copy-start.5
where the time goes:
time: 133 us
  starting transfers between devices  56.6 us (43%)
  waiting for transfers between devices  45.5 us (34%)
  Pallas kernels  21.7 us (16%)
  other arithmetic  4.76 us (4%)
  local copies, waits for them, and re-layouts  2.42 us (2%)
  between operations  1.54 us (1%)
    ppermute x10, starting transfers between devices, shift(): return lax.ppermute(x, axis, [(i, (i + by) % n) for i in range(n)])  28.9 us
    ppermute x10, waiting for transfers between devices, shift(): return lax.ppermute(x, axis, [(i, (i + by) % n) for i in range(n)])  26.9 us
    all_to_all x1, waiting for transfers between devices, local(): column = lax.all_to_all(staged, 'z', 0, 0, tiled=True)  12.2 us
    pallas_call x1, Pallas kernels, cross_attention(): pl.pallas_call(cross_body, grid=(steps,), out_shape=jax.ShapeDtypeStruct(...  10.4 us
    all_to_all x1, starting transfers between devices, local(): column = lax.all_to_all(staged, 'z', 0, 0, tiled=True)  10.3 us
    all_to_all x1, starting transfers between devices, local(): packed = lax.all_to_all(heads, ctx_axes, 0, 0, tiled=True)  8.08 us
    all_to_all x1, waiting for transfers between devices, local(): packed = lax.all_to_all(heads, ctx_axes, 0, 0, tiled=True)  6.37 us
    all_to_all x1, starting transfers between devices, local(): back = lax.all_to_all(head, ctx_axes, 0, 0, tiled=True)  5.72 us
  transfers between devices with their start and end apart: 14, of which 6 were waited for; matrix products, arithmetic and copies ran while one was open for 4% of the time, Pallas kernels for 7%

commit v1 on v0

--- a/solution.py
+++ b/solution.py
@@ -152,8 +152,8 @@
 
 
 def cross_body(pos_ref, *refs):
-    piece_refs, far_refs = refs[0:3], refs[3:5]
-    pick_ref, ka_ref, kb_ref, va_ref, vb_ref, q_ref, o_ref, rows_ref = refs[5:]
+    piece_refs = refs[:-8]
+    pick_ref, ka_ref, kb_ref, va_ref, vb_ref, q_ref, o_ref, rows_ref = refs[-8:]
     spans = q_ref.shape[1] // SPAN
     total = rows_ref.shape[0]
     each = total // spans
@@ -169,9 +169,6 @@
                 for s in range(spans):
                     at = s * each + p * rows
                     rows_ref[at : at + rows, cols] = part[s * rows : (s + 1) * rows].astype(BF)
-            for s, piece in enumerate(far_refs):
-                part = jnp.dot(piece[...], pick_ref[side], preferred_element_type=F32)
-                rows_ref[(s + 1) * each - part.shape[0] : (s + 1) * each, cols] = part.astype(BF)
 
     def project(a_ref, b_ref):
         return jnp.dot(rows_ref[:, :half], a_ref[...], preferred_element_type=F32) + jnp.dot(
@@ -204,8 +201,8 @@
             ).astype(BF)
 
 
-def cross_attention(pos, pieces, far, pick, own_w, other_w, queries):
-    total = sum(p.shape[0] for p in pieces) + sum(p.shape[0] for p in far)
+def cross_attention(pos, pieces, pick, own_w, other_w, queries):
+    total = sum(p.shape[0] for p in pieces)
     half, width = own_w.shape[0], own_w.shape[1] // 2
     wide = 2 * HD
     steps = width // wide
@@ -221,7 +218,6 @@
         in_specs=[
             pl.BlockSpec(memory_space=pltpu.SMEM),
             *[whole(x) for x in pieces],
-            *[whole(x) for x in far],
             whole(pick),
             key_block,
             key_block,
@@ -232,7 +228,7 @@
         out_specs=tokens,
         scratch_shapes=[pltpu.VMEM((total, 2 * half), BF)],
         name="cross_attention",
-    )(pos, *pieces, *far, pick, own_w, other_w, own_w, other_w, queries)
+    )(pos, *pieces, pick, own_w, other_w, own_w, other_w, queries)
 
 
 def shift(x, axis, by):
@@ -273,10 +269,8 @@
     mine = choose_rows(owner_ids, received)
     left = shift(mine, "mp", 1)
     right = shift(mine, "mp", -1)
-    mid = mine.shape[0] // 2
-    far_left = shift(left[:mid], "mp", 1)
-    far_right = shift(right[mid:], "mp", -1)
-    pieces, far = (mine, left, right), (far_left, far_right)
+    far = shift(mine, "mp", 2)
+    pieces = (mine, left, right, far)
 
     column = column.reshape(n_z * pad, 2 * width)
     beside = shift(column, "yl", 1)
@@ -308,7 +302,7 @@
     pick = (source[:, None, :] == entry).astype(BF)
 
     pos = jnp.stack([(x_at * n_y + y_at) * rows, lengths[0]]).astype(jnp.int32)
-    cross_core = cross_attention(pos, pieces, far, pick, own_w, other_w, cross_queries)
+    cross_core = cross_attention(pos, pieces, pick, own_w, other_w, cross_queries)
     return self_core, cross_core
 
 

time: 133 us -> 146 us (1.098)
  the two profiles are of different devices: /device:TPU:26 before, /device:TPU:11 now
where the time goes in v1:
time: 146 us; the launch traced here: 145 us
  starting transfers between devices  48.3 us (33%)
  waiting for transfers between devices  40.7 us (28%)
  blocking collectives  21.3 us (15%)
  Pallas kernels  21.1 us (14%)
  local copies, waits for them, and re-layouts  6.55 us (4%)
  other arithmetic  5.63 us (4%)
  between operations  1.49 us (1%)
    ppermute x9, starting transfers between devices, shift(): return lax.ppermute(x, axis, [(i, (i + by) % n) for i in range(n)])  32.2 us
    ppermute x9, waiting for transfers between devices, shift(): return lax.ppermute(x, axis, [(i, (i + by) % n) for i in range(n)])  29.7 us
    all_to_all x1, blocking collectives, local(): column = lax.all_to_all(staged, 'z', 0, 0, tiled=True)  21.3 us
    all_to_all x1, waiting for transfers between devices, local(): received = lax.all_to_all(offered, dp, 0, 0, tiled=True)  11 us
    pallas_call x1, Pallas kernels, cross_attention(): pl.pallas_call(cross_body, grid=(steps,), out_shape=jax.ShapeDtypeStruct(...  9.89 us
    all_to_all x1, starting transfers between devices, local(): back = lax.all_to_all(head, ctx_axes, 0, 0, tiled=True)  6.35 us
    unnamed x21, local copies, waits for them, and re-layouts  5.29 us
    all_to_all x1, starting transfers between devices, local(): packed = lax.all_to_all(heads, ctx_axes, 0, 0, tiled=True)  5.28 us
  transfers between devices with their start and end apart: 12, of which 5 were waited for; matrix products, arithmetic and copies ran while one was open for 6% of the time, Pallas kernels for 7%

profile of v1, /device:TPU:11, one launch (start us, length us, event | category | flops | bytes accessed | tf_op | source)
XLA Modules:
  0.0 145.0 jit_solution(18251409816596874922)
XLA Ops:
  0.6 0.8 pad_add_fusion.own_ref
  1.4 2.6 %collective-permute-start = (s32[1,2,4]{2,1,0:T(2,128)S(1)}, s32[1,2,4]{2,1,0:T(2,128)S(1)}, u32[]{:S(2)}, u32[]{:S(2)}) collective-permute-start(s32[1,2,4]{2,1,0:T(2,128)S(1)} %pad_add_fusion.own_ref), channel_id=1, source_target_pairs={{0,32},{32,0},{1,33},{33,1},{2,34},{34,2},{3,35},{35,3},{4,36},{36... | collective-permute-start | bytes 104 | tf_op jit(solution)/shard_map/ppermute | solution.py:236
  4.0 0.8 collective-permute-done.other_ref
  4.8 0.0 copy-done.6
  4.8 0.6 copy-done.7
  5.4 1.5 %stage_weights.1 = bf16[8,8,2048]{2,1,0:T(8,128)(2,1)} custom-call(s32[1,2,4]{2,1,0:T(2,128)} %copy-done.6, s32[1,2,4]{2,1,0:T(2,128)} %copy-done.7, bf16[7,1024]{1,0:T(8,128)(2,1)} %k_ref.3, bf16[7,1024]{1,0:T(8,128)(2,1)} %v_ref.3), custom_call_target="tpu_custom_call" | custom-call | tf_op jit(solution)/shard_map/stage_weights/pallas_call | solution.py:146
  6.8 21.3 %all_to_all.20 = bf16[8,8,2048]{2,1,0:T(8,128)(2,1)S(1)} all-to-all(bf16[8,8,2048]{2,1,0:T(8,128)(2,1)} %stage_weights.1), channel_id=1, replica_groups=mesh['z'=8,'core'=2,'x'=4,'yl'=2,'mp'=4] {'z'}, dimensions={0} | all-to-all | bytes 524288 | tf_op jit(solution)/shard_map/all_to_all | solution.py:263
  28.1 2.1 %collective-permute-start.4 = (bf16[64,2048]{1,0:T(8,128)(2,1)S(1)}, bf16[64,2048]{1,0:T(8,128)(2,1)S(1)}, u32[]{:S(2)}, u32[]{:S(2)}) collective-permute-start(bf16[64,2048]{1,0:T(8,128)(2,1)S(1)} %bitcast.11), channel_id=1, source_target_pairs={{0,4},{4,0},{1,5},{5,1},{2,6},{6,2},{3,7},{7,3},{8,12},{12,8},{9,1... | collective-permute-start | bytes 786440 | tf_op jit(solution)/shard_map/ppermute | solution.py:236
  30.2 2.1 %pack_heads.1 = bf16[8,3,128,128]{3,2,1,0:T(8,128)(2,1)} custom-call(bf16[1,128,1024]{2,1,0:T(8,128)(2,1)} %q_ref.1, bf16[1,128,1024]{2,1,0:T(8,128)(2,1)} %k_ref.2, bf16[1,128,1024]{2,1,0:T(8,128)(2,1)} %v_ref.2), custom_call_target="tpu_custom_call" | custom-call | tf_op jit(solution)/shard_map/pack_heads/pallas_call | solution.py:30
  32.3 5.3 %all-to-all-start = ((bf16[8,3,128,128]{3,2,1,0:T(8,128)(2,1)}), bf16[8,3,128,128]{3,2,1,0:T(8,128)(2,1)S(1)}, u32[]{:S(2)}, u32[]{:S(2)}) async-start(bf16[8,3,128,128]{3,2,1,0:T(8,128)(2,1)} %pack_heads.1), calls=%async_computation | async-start | bytes 1572864 | tf_op jit(solution)/shard_map/all_to_all | solution.py:285
  37.6 0.7 pad_add_fusion.2.where_ref
  38.3 0.0 collective-permute-done.4
  38.3 0.8 pad_maximum_fusion
  39.1 3.1 %collective-permute-start.5 = (bf16[128,2048]{1,0:T(8,128)(2,1)}, bf16[128,2048]{1,0:T(8,128)(2,1)}, u32[]{:S(2)}, u32[]{:S(2)}) collective-permute-start(bf16[128,2048]{1,0:T(8,128)(2,1)} %pad_maximum_fusion), channel_id=1, source_target_pairs={{0,8},{8,16},{16,24},{24,0},{1,9},{9,17},{17,25},{25,1},{2,10},{10... | collective-permute-start | bytes 1572872 | tf_op jit(solution)/shard_map/ppermute | solution.py:236
  42.2 2.2 %collective-permute-start.6 = (bf16[128,2048]{1,0:T(8,128)(2,1)}, bf16[128,2048]{1,0:T(8,128)(2,1)}, u32[]{:S(2)}, u32[]{:S(2)}) collective-permute-start(bf16[128,2048]{1,0:T(8,128)(2,1)} %pad_maximum_fusion), channel_id=1, source_target_pairs={{0,24},{8,0},{16,8},{24,16},{1,25},{9,1},{17,9},{25,17},{2,26},{10... | collective-permute-start | bytes 1572872 | tf_op jit(solution)/shard_map/ppermute | solution.py:236
  44.4 0.6 slice_convert_fusion
  45.0 2.3 %offer_rows.1 = bf16[16,32,896]{2,1,0:T(8,128)(2,1)} custom-call(s32[8,16]{1,0:T(8,128)} %bitcast.16, s32[3]{0:T(128)} %pad_add_fusion.2.where_ref, bf16[512,896]{1,0:T(8,128)(2,1)} %bitcast.15), custom_call_target="tpu_custom_call" | custom-call | tf_op jit(solution)/shard_map/offer_rows/pallas_call | solution.py:87
  47.3 10.8 %collective-permute-done.5 = bf16[128,2048]{1,0:T(8,128)(2,1)} collective-permute-done((bf16[128,2048]{1,0:T(8,128)(2,1)}, bf16[128,2048]{1,0:T(8,128)(2,1)}, u32[]{:S(2)}, u32[]{:S(2)}) %collective-permute-start.5) | collective-permute-done | bytes 524320 | tf_op jit(solution)/shard_map/ppermute | solution.py:236
  58.1 3.8 %collective-permute-start.7 = (bf16[128,2048]{1,0:T(8,128)(2,1)}, bf16[128,2048]{1,0:T(8,128)(2,1)}, u32[]{:S(2)}, u32[]{:S(2)}) collective-permute-start(bf16[128,2048]{1,0:T(8,128)(2,1)} %collective-permute-done.5), channel_id=1, source_target_pairs={{0,8},{8,16},{16,24},{24,0},{1,9},{9,17},{17,25},{25,1},{2,10},{10... | collective-permute-start | bytes 1572872 | tf_op jit(solution)/shard_map/ppermute | solution.py:236
  61.9 1.1 constant_dynamic-update-slice_fusion.2
  63.1 0.0 collective-permute-done.6
  63.1 1.1 constant_dynamic-update-slice_fusion.1
  64.2 0.0 all-to-all-done.x_ref
  64.2 0.9 copy-done.2
  65.1 4.4 %all-to-all-start.3 = ((bf16[16,32,896]{2,1,0:T(8,128)(2,1)}), bf16[16,32,896]{2,1,0:T(8,128)(2,1)S(1)}, u32[]{:S(2)}, u32[]{:S(2)}) async-start(bf16[16,32,896]{2,1,0:T(8,128)(2,1)} %offer_rows.1), calls=%async_computation.3 | async-start | bytes 1835008 | tf_op jit(solution)/shard_map/all_to_all | solution.py:268
  69.5 4.6 %collective-permute-done.7 = bf16[128,2048]{1,0:T(8,128)(2,1)} collective-permute-done((bf16[128,2048]{1,0:T(8,128)(2,1)}, bf16[128,2048]{1,0:T(8,128)(2,1)}, u32[]{:S(2)}, u32[]{:S(2)}) %collective-permute-start.7) | collective-permute-done | bytes 524320 | tf_op jit(solution)/shard_map/ppermute | solution.py:236
  74.1 1.1 constant_dynamic-update-slice_fusion.refs_5_.refs_7_
  75.2 3.8 %collective-permute-start.8 = (bf16[512,2048]{1,0:T(8,128)(2,1)S(1)}, bf16[512,2048]{1,0:T(8,128)(2,1)}, u32[]{:S(2)}, u32[]{:S(2)}) collective-permute-start(bf16[512,2048]{1,0:T(8,128)(2,1)S(1)} %constant_dynamic-update-slice_fusion.refs_5_.refs_7_), channel_id=1, source_target_pairs={{0,32},{32,0},{1,33},{33,1},{2,34},{34,2},{3,35},{35,3},{4,36},{36... | collective-permute-start | bytes 6291464 | tf_op jit(solution)/shard_map/ppermute | solution.py:236
  79.7 0.1 pad_add_fusion.3
  79.7 0.7 pad_add_fusion.1.pos_ref
  80.4 3.4 %self_attention.1 = bf16[8,128,128]{2,1,0:T(8,128)(2,1)} custom-call(s32[1]{0:T(128)S(6)} %copy.18.len_ref, bf16[8,3,128,128]{3,2,1,0:T(8,128)(2,1)} %copy-done.2), custom_call_target="tpu_custom_call" | custom-call | tf_op jit(solution)/shard_map/self_attention/pallas_call | solution.py:59
  83.9 11.0 %all-to-all-done.3.x_ref = bf16[16,32,896]{2,1,0:T(8,128)(2,1)S(1)} async-done(((bf16[16,32,896]{2,1,0:T(8,128)(2,1)}), bf16[16,32,896]{2,1,0:T(8,128)(2,1)S(1)}, u32[]{:S(2)}, u32[]{:S(2)}) %all-to-all-start.3) | async-done | bytes 917536 | tf_op jit(solution)/shard_map/all_to_all | solution.py:268
  94.9 6.4 %all-to-all-start.1 = ((bf16[8,128,128]{2,1,0:T(8,128)(2,1)}), bf16[8,128,128]{2,1,0:T(8,128)(2,1)S(1)}, u32[]{:S(2)}, u32[]{:S(2)}) async-start(bf16[8,128,128]{2,1,0:T(8,128)(2,1)} %self_attention.1), calls=%async_computation.1 | async-start | bytes 524288 | tf_op jit(solution)/shard_map/all_to_all | solution.py:287
  101.2 0.1 add_select_fusion
  101.3 1.9 %choose_rows.1.refs_0_ = bf16[128,896]{1,0:T(8,128)(2,1)} custom-call(s32[1,2,2]{2,1,0:T(2,128)} %own_ref.1, bf16[16,32,896]{2,1,0:T(8,128)(2,1)} %copy-done.1), custom_call_target="tpu_custom_call" | custom-call | tf_op jit(solution)/shard_map/choose_rows/pallas_call | solution.py:108
  103.2 4.2 %collective-permute-start.1 = (bf16[128,896]{1,0:T(8,128)(2,1)}, bf16[128,896]{1,0:T(8,128)(2,1)S(1)}, u32[]{:S(2)}, u32[]{:S(2)}) collective-permute-start(bf16[128,896]{1,0:T(8,128)(2,1)} %choose_rows.1.refs_0_), channel_id=1, source_target_pairs={{0,1},{1,2},{2,3},{3,0},{4,5},{5,6},{6,7},{7,4},{8,9},{9,10},{10,1... | collective-permute-start | bytes 688136 | tf_op jit(solution)/shard_map/ppermute | solution.py:236
  107.4 3.5 %collective-permute-start.2 = (bf16[128,896]{1,0:T(8,128)(2,1)}, bf16[128,896]{1,0:T(8,128)(2,1)S(1)}, u32[]{:S(2)}, u32[]{:S(2)}) collective-permute-start(bf16[128,896]{1,0:T(8,128)(2,1)} %choose_rows.1.refs_0_), channel_id=1, source_target_pairs={{0,3},{1,0},{2,1},{3,2},{4,7},{5,4},{6,5},{7,6},{8,11},{9,8},{10,9... | collective-permute-start | bytes 688136 | tf_op jit(solution)/shard_map/ppermute | solution.py:236
  110.9 7.0 %collective-permute-start.3 = (bf16[128,896]{1,0:T(8,128)(2,1)}, bf16[128,896]{1,0:T(8,128)(2,1)S(1)}, u32[]{:S(2)}, u32[]{:S(2)}) collective-permute-start(bf16[128,896]{1,0:T(8,128)(2,1)} %choose_rows.1.refs_0_), channel_id=1, source_target_pairs={{0,2},{1,3},{2,0},{3,1},{4,6},{5,7},{6,4},{7,5},{8,10},{9,11},{10,... | collective-permute-start | bytes 688136 | tf_op jit(solution)/shard_map/ppermute | solution.py:236
  117.9 1.9 %fusion.refs_4_ = bf16[2,896,512]{2,1,0:T(8,128)(2,1)} fusion(s32[2,512]{1,0:T(2,128)S(1)} %add_select_fusion), kind=kLoop, calls=%fused_computation.1 | loop fusion | flops 1835008 | bytes 1839104 | tf_op jit(solution)/shard_map/convert_element_type | solution.py:302
  119.9 0.0 all-to-all-done.1
  119.9 0.2 copy.12
  120.1 0.9 copy.13
  120.9 0.0 collective-permute-done.1.refs_1_
  120.9 0.0 collective-permute-done.2.refs_2_
  120.9 13.5 %collective-permute-done.3.refs_3_ = bf16[128,896]{1,0:T(8,128)(2,1)S(1)} collective-permute-done((bf16[128,896]{1,0:T(8,128)(2,1)}, bf16[128,896]{1,0:T(8,128)(2,1)S(1)}, u32[]{:S(2)}, u32[]{:S(2)}) %collective-permute-start.3) | collective-permute-done | bytes 229408 | tf_op jit(solution)/shard_map/ppermute | solution.py:236
  134.4 0.0 collective-permute-done.8.refs_6_.refs_8_
  134.4 0.7 copy-done.5
  135.1 9.9 %cross_attention.1 = bf16[1,128,1024]{2,1,0:T(8,128)(2,1)} custom-call(s32[2]{0:T(128)} %pad_add_fusion.1.pos_ref, bf16[128,896]{1,0:T(8,128)(2,1)} %choose_rows.1.refs_0_, bf16[128,896]{1,0:T(8,128)(2,1)} %copy-done.3, bf16[128,896]{1,0:T(8,128)(2,1)} %copy-done.4, bf16[128,896]{1,0:T(8,128)(2,1)} %copy-done.5, bf16[2,896,512]{2,1,0:T(8,128)(2,1)} %fusion.refs_4_, ...), custom_call_target="tpu_custom_call" | custom-call | tf_op jit(solution)/shard_map/cross_attention/pallas_call | solution.py:214
  (17 shorter events, 0.1 us)
Async XLA Ops:
  1.4 3.4 %copy-start.6 = (s32[1,2,4]{2,1,0:T(2,128)}, s32[1,2,4]{2,1,0:T(2,128)S(1)}, u32[]{:S(2)}) copy-start(s32[1,2,4]{2,1,0:T(2,128)S(1)} %pad_add_fusion.own_ref) | copy-start | bytes 100
  1.4 3.4 %collective-permute-start = (s32[1,2,4]{2,1,0:T(2,128)S(1)}, s32[1,2,4]{2,1,0:T(2,128)S(1)}, u32[]{:S(2)}, u32[]{:S(2)}) collective-permute-start(s32[1,2,4]{2,1,0:T(2,128)S(1)} %pad_add_fusion.own_ref), channel_id=1, source_target_pairs={{0,32},{32,0},{1,33},{33,1},{2,34},{34,2},{3,35},{35,3},{4,36},{36... | collective-permute-start | bytes 104 | tf_op jit(solution)/shard_map/ppermute | solution.py:236
  4.8 0.6 copy-start.7
  28.1 10.2 %collective-permute-start.4 = (bf16[64,2048]{1,0:T(8,128)(2,1)S(1)}, bf16[64,2048]{1,0:T(8,128)(2,1)S(1)}, u32[]{:S(2)}, u32[]{:S(2)}) collective-permute-start(bf16[64,2048]{1,0:T(8,128)(2,1)S(1)} %bitcast.11), channel_id=1, source_target_pairs={{0,4},{4,0},{1,5},{5,1},{2,6},{6,2},{3,7},{7,3},{8,12},{12,8},{9,1... | collective-permute-start | bytes 786440 | tf_op jit(solution)/shard_map/ppermute | solution.py:236
  32.3 31.8 %all-to-all-start = ((bf16[8,3,128,128]{3,2,1,0:T(8,128)(2,1)}), bf16[8,3,128,128]{3,2,1,0:T(8,128)(2,1)S(1)}, u32[]{:S(2)}, u32[]{:S(2)}) async-start(bf16[8,3,128,128]{3,2,1,0:T(8,128)(2,1)} %pack_heads.1), calls=%async_computation | async-start | bytes 1572864 | tf_op jit(solution)/shard_map/all_to_all | solution.py:285
  39.1 19.0 %collective-permute-start.5 = (bf16[128,2048]{1,0:T(8,128)(2,1)}, bf16[128,2048]{1,0:T(8,128)(2,1)}, u32[]{:S(2)}, u32[]{:S(2)}) collective-permute-start(bf16[128,2048]{1,0:T(8,128)(2,1)} %pad_maximum_fusion), channel_id=1, source_target_pairs={{0,8},{8,16},{16,24},{24,0},{1,9},{9,17},{17,25},{25,1},{2,10},{10... | collective-permute-start | bytes 1572872 | tf_op jit(solution)/shard_map/ppermute | solution.py:236
  42.2 20.8 %collective-permute-start.6 = (bf16[128,2048]{1,0:T(8,128)(2,1)}, bf16[128,2048]{1,0:T(8,128)(2,1)}, u32[]{:S(2)}, u32[]{:S(2)}) collective-permute-start(bf16[128,2048]{1,0:T(8,128)(2,1)} %pad_maximum_fusion), channel_id=1, source_target_pairs={{0,24},{8,0},{16,8},{24,16},{1,25},{9,1},{17,9},{25,17},{2,26},{10... | collective-permute-start | bytes 1572872 | tf_op jit(solution)/shard_map/ppermute | solution.py:236
  58.1 16.0 %collective-permute-start.7 = (bf16[128,2048]{1,0:T(8,128)(2,1)}, bf16[128,2048]{1,0:T(8,128)(2,1)}, u32[]{:S(2)}, u32[]{:S(2)}) collective-permute-start(bf16[128,2048]{1,0:T(8,128)(2,1)} %collective-permute-done.5), channel_id=1, source_target_pairs={{0,8},{8,16},{16,24},{24,0},{1,9},{9,17},{17,25},{25,1},{2,10},{10... | collective-permute-start | bytes 1572872 | tf_op jit(solution)/shard_map/ppermute | solution.py:236
  64.2 0.9 copy-start.2
  65.1 29.8 %all-to-all-start.3 = ((bf16[16,32,896]{2,1,0:T(8,128)(2,1)}), bf16[16,32,896]{2,1,0:T(8,128)(2,1)S(1)}, u32[]{:S(2)}, u32[]{:S(2)}) async-start(bf16[16,32,896]{2,1,0:T(8,128)(2,1)} %offer_rows.1), calls=%async_computation.3 | async-start | bytes 1835008 | tf_op jit(solution)/shard_map/all_to_all | solution.py:268
  75.2 44.7 %copy-start = (bf16[512,2048]{1,0:T(8,128)(2,1)}, bf16[512,2048]{1,0:T(8,128)(2,1)S(1)}, u32[]{:S(2)}) copy-start(bf16[512,2048]{1,0:T(8,128)(2,1)S(1)} %constant_dynamic-update-slice_fusion.refs_5_.refs_7_) | copy-start | bytes 6291460
  75.2 59.2 %collective-permute-start.8 = (bf16[512,2048]{1,0:T(8,128)(2,1)S(1)}, bf16[512,2048]{1,0:T(8,128)(2,1)}, u32[]{:S(2)}, u32[]{:S(2)}) collective-permute-start(bf16[512,2048]{1,0:T(8,128)(2,1)S(1)} %constant_dynamic-update-slice_fusion.refs_5_.refs_7_), channel_id=1, source_target_pairs={{0,32},{32,0},{1,33},{33,1},{2,34},{34,2},{3,35},{35,3},{4,36},{36... | collective-permute-start | bytes 6291464 | tf_op jit(solution)/shard_map/ppermute | solution.py:236
  94.9 6.4 %copy-start.1 = (bf16[16,32,896]{2,1,0:T(8,128)(2,1)}, bf16[16,32,896]{2,1,0:T(8,128)(2,1)S(1)}, u32[]{:S(2)}) copy-start(bf16[16,32,896]{2,1,0:T(8,128)(2,1)S(1)} %all-to-all-done.3.x_ref) | copy-start | bytes 2752516
  94.9 25.0 %all-to-all-start.1 = ((bf16[8,128,128]{2,1,0:T(8,128)(2,1)}), bf16[8,128,128]{2,1,0:T(8,128)(2,1)S(1)}, u32[]{:S(2)}, u32[]{:S(2)}) async-start(bf16[8,128,128]{2,1,0:T(8,128)(2,1)} %self_attention.1), calls=%async_computation.1 | async-start | bytes 524288 | tf_op jit(solution)/shard_map/all_to_all | solution.py:287
  103.2 17.7 %collective-permute-start.1 = (bf16[128,896]{1,0:T(8,128)(2,1)}, bf16[128,896]{1,0:T(8,128)(2,1)S(1)}, u32[]{:S(2)}, u32[]{:S(2)}) collective-permute-start(bf16[128,896]{1,0:T(8,128)(2,1)} %choose_rows.1.refs_0_), channel_id=1, source_target_pairs={{0,1},{1,2},{2,3},{3,0},{4,5},{5,6},{6,7},{7,4},{8,9},{9,10},{10,1... | collective-permute-start | bytes 688136 | tf_op jit(solution)/shard_map/ppermute | solution.py:236
  107.4 13.5 %collective-permute-start.2 = (bf16[128,896]{1,0:T(8,128)(2,1)}, bf16[128,896]{1,0:T(8,128)(2,1)S(1)}, u32[]{:S(2)}, u32[]{:S(2)}) collective-permute-start(bf16[128,896]{1,0:T(8,128)(2,1)} %choose_rows.1.refs_0_), channel_id=1, source_target_pairs={{0,3},{1,0},{2,1},{3,2},{4,7},{5,4},{6,5},{7,6},{8,11},{9,8},{10,9... | collective-permute-start | bytes 688136 | tf_op jit(solution)/shard_map/ppermute | solution.py:236
  110.9 23.5 %collective-permute-start.3 = (bf16[128,896]{1,0:T(8,128)(2,1)}, bf16[128,896]{1,0:T(8,128)(2,1)S(1)}, u32[]{:S(2)}, u32[]{:S(2)}) collective-permute-start(bf16[128,896]{1,0:T(8,128)(2,1)} %choose_rows.1.refs_0_), channel_id=1, source_target_pairs={{0,2},{1,3},{2,0},{3,1},{4,6},{5,7},{6,4},{7,5},{8,10},{9,11},{10,... | collective-permute-start | bytes 688136 | tf_op jit(solution)/shard_map/ppermute | solution.py:236
  120.9 13.5 %copy-start.3 = (bf16[128,896]{1,0:T(8,128)(2,1)}, bf16[128,896]{1,0:T(8,128)(2,1)S(1)}, u32[]{:S(2)}) copy-start(bf16[128,896]{1,0:T(8,128)(2,1)S(1)} %collective-permute-done.1.refs_1_) | copy-start | bytes 688132
  120.9 13.5 %copy-start.4 = (bf16[128,896]{1,0:T(8,128)(2,1)}, bf16[128,896]{1,0:T(8,128)(2,1)S(1)}, u32[]{:S(2)}) copy-start(bf16[128,896]{1,0:T(8,128)(2,1)S(1)} %collective-permute-done.2.refs_2_) | copy-start | bytes 688132
  134.4 0.7 copy-start.5

commit v2 on v1

--- a/solution.py
+++ b/solution.py
@@ -176,29 +176,36 @@
         )
 
     key_proj = project(ka_ref, kb_ref)
-    value_proj = project(va_ref, vb_ref).astype(BF)
+    heads = [slice(h * HD, (h + 1) * HD) for h in range(o_ref.shape[2] // HD)]
+    keys = []
+    for cols in heads:
+        head = key_proj[:, cols]
+        scale = lax.rsqrt(jnp.mean(head * head, axis=1, keepdims=True) + 1e-06)
+        keys.append((head * scale).astype(BF))
+    values = project(va_ref, vb_ref).astype(BF)
     start, length = pos_ref[0], pos_ref[1]
-    for h in range(o_ref.shape[2] // HD):
-        cols = slice(h * HD, (h + 1) * HD)
-        keys = key_proj[:, cols]
-        scale = lax.rsqrt(jnp.mean(keys * keys, axis=1, keepdims=True) + 1e-06)
-        keys = (keys * scale).astype(BF)
-        values = value_proj[:, cols]
-        for s in range(spans):
-            own = slice(s * each, (s + 1) * each)
-            scores = lax.dot_general(
-                q_ref[0, s * SPAN : (s + 1) * SPAN, cols],
-                keys[own],
-                NT,
-                preferred_element_type=F32,
-            ) * SCALE
-            weights = jnp.exp(scores)
-            sums = jnp.dot(weights.astype(BF), values[own], preferred_element_type=F32)
-            result = sums / jnp.sum(weights, axis=1, keepdims=True)
-            place = lax.broadcasted_iota(jnp.int32, (SPAN, HD), 0) + (start + s * SPAN)
-            o_ref[0, s * SPAN : (s + 1) * SPAN, cols] = jnp.where(
-                place < length, result, 0.0
-            ).astype(BF)
+    places = [(h, s) for h in range(len(heads)) for s in range(spans)]
+    token = lambda s: slice(s * SPAN, (s + 1) * SPAN)
+    own = lambda s: slice(s * each, (s + 1) * each)
+    weights = [
+        jnp.exp(
+            lax.dot_general(
+                q_ref[0, token(s), heads[h]], keys[h][own(s)], NT, preferred_element_type=F32
+            )
+            * SCALE
+        )
+        for h, s in places
+    ]
+    sums = [
+        jnp.dot(w.astype(BF), values[own(s), heads[h]], preferred_element_type=F32)
+        for w, (h, s) in zip(weights, places)
+    ]
+    totals = [jnp.sum(w, axis=1, keepdims=True) for w in weights]
+    for top, total_weight, (h, s) in zip(sums, totals, places):
+        place = lax.broadcasted_iota(jnp.int32, (SPAN, HD), 0) + (start + s * SPAN)
+        o_ref[0, token(s), heads[h]] = jnp.where(
+            place < length, top / total_weight, 0.0
+        ).astype(BF)
 
 
 def cross_attention(pos, pieces, pick, own_w, other_w, queries):
@@ -278,12 +285,12 @@
     w_left = shift(column, "x", 1)
     w_right = shift(column, "x", -1)
     w_far = shift(w_left, "x", 1)
-    own_w = jnp.concatenate([column, w_left, w_right, w_far], axis=0)
-    other_w = shift(own_w, "core", 1)
-
     heads = pack_heads(queries, keys, values)
     packed = lax.all_to_all(heads, ctx_axes, 0, 0, tiled=True)
     head = self_attention(lengths, packed)
+    column, w_left, w_right, head = lax.optimization_barrier((column, w_left, w_right, head))
+    own_w = jnp.concatenate([column, w_left, w_right, w_far], axis=0)
+    other_w = shift(own_w, "core", 1)
     back = lax.all_to_all(head, ctx_axes, 0, 0, tiled=True)
     self_core = jnp.transpose(back, (1, 0, 2)).reshape(1, rows, width)
 

time: 146 us -> 145 us (level)
  blocking collectives: 21.3 us -> 0 us
  waiting for transfers between devices: 40.7 us -> 54 us
  starting transfers between devices: 48.3 us -> 57.5 us
    all_to_all x1 -> x0, blocking collectives: 21.3 us -> none  [local(): column = lax.all_to_all(staged, 'z', 0, 0, tiled=True)]
    all_to_all x0 -> x1, starting transfers between devices: none -> 10 us  [local(): column = lax.all_to_all(staged, 'z', 0, 0, tiled=True)]
    all_to_all x0 -> x1, waiting for transfers between devices: none -> 9.11 us  [local(): column = lax.all_to_all(staged, 'z', 0, 0, tiled=True)]
    all_to_all x1, waiting for transfers between devices: 11 us -> 15.2 us  [local(): received = lax.all_to_all(offered, dp, 0, 0, tiled=True)]
    all_to_all x1, starting transfers between devices: 4.38 us -> 7.26 us  [local(): received = lax.all_to_all(offered, dp, 0, 0, tiled=True)]
    ppermute x9, starting transfers between devices: 32.2 us -> 29.9 us  [shift(): return lax.ppermute(x, axis, [(i, (i + by) % n) for i in range(n)])]
    unnamed x21 -> x20, local copies, waits for them, and re-layouts: 5.29 us -> 4.35 us
  transfers between devices with their start and end apart: 12 -> 13, of which waited for: 5 -> 7; matrix products, arithmetic and copies ran while one was open for 6% -> 6% of each run, Pallas kernels for 7% -> 7%
where the time goes in v2:
time: 145 us; the launch traced here: 143 us
  starting transfers between devices  57.5 us (40%)
  waiting for transfers between devices  54 us (37%)
  Pallas kernels  20.1 us (14%)
  local copies, waits for them, and re-layouts  5.6 us (4%)
  other arithmetic  4.77 us (3%)
  between operations  1.47 us (1%)
    ppermute x9, starting transfers between devices, shift(): return lax.ppermute(x, axis, [(i, (i + by) % n) for i in range(n)])  29.9 us
    ppermute x9, waiting for transfers between devices, shift(): return lax.ppermute(x, axis, [(i, (i + by) % n) for i in range(n)])  29.7 us
    all_to_all x1, waiting for transfers between devices, local(): received = lax.all_to_all(offered, dp, 0, 0, tiled=True)  15.2 us
    all_to_all x1, starting transfers between devices, local(): column = lax.all_to_all(staged, 'z', 0, 0, tiled=True)  10 us
    all_to_all x1, waiting for transfers between devices, local(): column = lax.all_to_all(staged, 'z', 0, 0, tiled=True)  9.11 us
    pallas_call x1, Pallas kernels, cross_attention(): pl.pallas_call(cross_body, grid=(steps,), out_shape=jax.ShapeDtypeStruct(...  8.85 us
    all_to_all x1, starting transfers between devices, local(): received = lax.all_to_all(offered, dp, 0, 0, tiled=True)  7.26 us
    all_to_all x1, starting transfers between devices, local(): packed = lax.all_to_all(heads, ctx_axes, 0, 0, tiled=True)  5.17 us
  transfers between devices with their start and end apart: 13, of which 7 were waited for; matrix products, arithmetic and copies ran while one was open for 6% of the time, Pallas kernels for 7%

profile of v2, /device:TPU:11, one launch (start us, length us, event | category | flops | bytes accessed | tf_op | source)
XLA Modules:
  0.0 143.4 jit_solution(8434731875163802176)
XLA Ops:
  0.6 0.8 pad_add_fusion.own_ref
  1.4 2.6 %collective-permute-start = (s32[1,2,4]{2,1,0:T(2,128)S(1)}, s32[1,2,4]{2,1,0:T(2,128)S(1)}, u32[]{:S(2)}, u32[]{:S(2)}) collective-permute-start(s32[1,2,4]{2,1,0:T(2,128)S(1)} %pad_add_fusion.own_ref), channel_id=1, source_target_pairs={{0,32},{32,0},{1,33},{33,1},{2,34},{34,2},{3,35},{35,3},{4,36},{36... | collective-permute-start | bytes 104 | tf_op jit(solution)/shard_map/ppermute | solution.py:243
  4.0 0.8 collective-permute-done.other_ref
  4.8 0.0 copy-done.6
  4.8 0.6 copy-done.7
  5.4 1.5 %stage_weights.1 = bf16[8,8,2048]{2,1,0:T(8,128)(2,1)} custom-call(s32[1,2,4]{2,1,0:T(2,128)} %copy-done.6, s32[1,2,4]{2,1,0:T(2,128)} %copy-done.7, bf16[7,1024]{1,0:T(8,128)(2,1)} %k_ref.2, bf16[7,1024]{1,0:T(8,128)(2,1)} %v_ref.2), custom_call_target="tpu_custom_call" | custom-call | tf_op jit(solution)/shard_map/stage_weights/pallas_call | solution.py:146
  6.9 10.0 %all-to-all-start = ((bf16[8,8,2048]{2,1,0:T(8,128)(2,1)}), bf16[8,8,2048]{2,1,0:T(8,128)(2,1)S(1)}, u32[]{:S(2)}, u32[]{:S(2)}) async-start(bf16[8,8,2048]{2,1,0:T(8,128)(2,1)} %stage_weights.1), calls=%async_computation | async-start | bytes 524288 | tf_op jit(solution)/shard_map/all_to_all | solution.py:270
  16.9 2.1 %pack_heads.1 = bf16[8,3,128,128]{3,2,1,0:T(8,128)(2,1)} custom-call(bf16[1,128,1024]{2,1,0:T(8,128)(2,1)} %q_ref.1, bf16[1,128,1024]{2,1,0:T(8,128)(2,1)} %k_ref.3, bf16[1,128,1024]{2,1,0:T(8,128)(2,1)} %v_ref.3), custom_call_target="tpu_custom_call" | custom-call | tf_op jit(solution)/shard_map/pack_heads/pallas_call | solution.py:30
  19.0 9.1 %all-to-all-done = bf16[8,8,2048]{2,1,0:T(8,128)(2,1)S(1)} async-done(((bf16[8,8,2048]{2,1,0:T(8,128)(2,1)}), bf16[8,8,2048]{2,1,0:T(8,128)(2,1)S(1)}, u32[]{:S(2)}, u32[]{:S(2)}) %all-to-all-start) | async-done | bytes 262176 | tf_op jit(solution)/shard_map/all_to_all | solution.py:270
  28.1 5.2 %all-to-all-start.1 = ((bf16[8,3,128,128]{3,2,1,0:T(8,128)(2,1)}), bf16[8,3,128,128]{3,2,1,0:T(8,128)(2,1)S(1)}, u32[]{:S(2)}, u32[]{:S(2)}) async-start(bf16[8,3,128,128]{3,2,1,0:T(8,128)(2,1)} %pack_heads.1), calls=%async_computation.1 | async-start | bytes 1572864 | tf_op jit(solution)/shard_map/all_to_all | solution.py:289
  33.3 2.2 %collective-permute-start.1 = (bf16[64,2048]{1,0:T(8,128)(2,1)S(1)}, bf16[64,2048]{1,0:T(8,128)(2,1)S(1)}, u32[]{:S(2)}, u32[]{:S(2)}) collective-permute-start(bf16[64,2048]{1,0:T(8,128)(2,1)S(1)} %bitcast.10), channel_id=1, source_target_pairs={{0,4},{4,0},{1,5},{5,1},{2,6},{6,2},{3,7},{7,3},{8,12},{12,8},{9,1... | collective-permute-start | bytes 786440 | tf_op jit(solution)/shard_map/ppermute | solution.py:243
  35.5 11.3 %collective-permute-done.1 = bf16[64,2048]{1,0:T(8,128)(2,1)S(1)} collective-permute-done((bf16[64,2048]{1,0:T(8,128)(2,1)S(1)}, bf16[64,2048]{1,0:T(8,128)(2,1)S(1)}, u32[]{:S(2)}, u32[]{:S(2)}) %collective-permute-start.1) | collective-permute-done | bytes 262176 | tf_op jit(solution)/shard_map/ppermute | solution.py:243
  46.8 3.1 %collective-permute-start.2 = (bf16[128,2048]{1,0:T(8,128)(2,1)S(1)}, bf16[128,2048]{1,0:T(8,128)(2,1)}, u32[]{:S(2)}, u32[]{:S(2)}) collective-permute-start(bf16[128,2048]{1,0:T(8,128)(2,1)S(1)} %pad_maximum_fusion), channel_id=1, source_target_pairs={{0,8},{8,16},{16,24},{24,0},{1,9},{9,17},{17,25},{25,1},{2,10},{10... | collective-permute-start | bytes 1572872 | tf_op jit(solution)/shard_map/ppermute | solution.py:243
  50.0 2.1 %collective-permute-start.3 = (bf16[128,2048]{1,0:T(8,128)(2,1)S(1)}, bf16[128,2048]{1,0:T(8,128)(2,1)}, u32[]{:S(2)}, u32[]{:S(2)}) collective-permute-start(bf16[128,2048]{1,0:T(8,128)(2,1)S(1)} %pad_maximum_fusion), channel_id=1, source_target_pairs={{0,24},{8,0},{16,8},{24,16},{1,25},{9,1},{17,9},{25,17},{2,26},{10... | collective-permute-start | bytes 1572872 | tf_op jit(solution)/shard_map/ppermute | solution.py:243
  52.8 0.6 pad_add_fusion.2.where_ref
  53.4 0.6 slice_convert_fusion
  54.0 2.3 %offer_rows.1 = bf16[16,32,896]{2,1,0:T(8,128)(2,1)} custom-call(s32[8,16]{1,0:T(8,128)} %bitcast.15, s32[3]{0:T(128)} %pad_add_fusion.2.where_ref, bf16[512,896]{1,0:T(8,128)(2,1)} %bitcast.14), custom_call_target="tpu_custom_call" | custom-call | tf_op jit(solution)/shard_map/offer_rows/pallas_call | solution.py:87
  56.3 3.2 %collective-permute-done.2 = bf16[128,2048]{1,0:T(8,128)(2,1)} collective-permute-done((bf16[128,2048]{1,0:T(8,128)(2,1)S(1)}, bf16[128,2048]{1,0:T(8,128)(2,1)}, u32[]{:S(2)}, u32[]{:S(2)}) %collective-permute-start.2) | collective-permute-done | bytes 524320 | tf_op jit(solution)/shard_map/ppermute | solution.py:243
  59.6 3.2 %collective-permute-start.7 = (bf16[128,2048]{1,0:T(8,128)(2,1)}, bf16[128,2048]{1,0:T(8,128)(2,1)}, u32[]{:S(2)}, u32[]{:S(2)}) collective-permute-start(bf16[128,2048]{1,0:T(8,128)(2,1)} %collective-permute-done.2), channel_id=1, source_target_pairs={{0,8},{8,16},{16,24},{24,0},{1,9},{9,17},{17,25},{25,1},{2,10},{10... | collective-permute-start | bytes 1572872 | tf_op jit(solution)/shard_map/ppermute | solution.py:243
  62.8 0.0 all-to-all-done.1.x_ref
  62.8 7.3 %all-to-all-start.3 = ((bf16[16,32,896]{2,1,0:T(8,128)(2,1)}), bf16[16,32,896]{2,1,0:T(8,128)(2,1)S(1)}, u32[]{:S(2)}, u32[]{:S(2)}) async-start(bf16[16,32,896]{2,1,0:T(8,128)(2,1)} %offer_rows.1), calls=%async_computation.3 | async-start | bytes 1835008 | tf_op jit(solution)/shard_map/all_to_all | solution.py:275
  70.1 3.4 %self_attention.1 = bf16[8,128,128]{2,1,0:T(8,128)(2,1)} custom-call(s32[1]{0:T(128)S(6)} %copy.17.len_ref, bf16[8,3,128,128]{3,2,1,0:T(8,128)(2,1)} %copy-done.2), custom_call_target="tpu_custom_call" | custom-call | tf_op jit(solution)/shard_map/self_attention/pallas_call | solution.py:59
  73.5 0.0 collective-permute-done.3
  73.5 1.1 constant_dynamic-update-slice_fusion.2
  74.6 1.1 constant_dynamic-update-slice_fusion.1
  75.7 0.0 collective-permute-done.7
  75.7 1.1 constant_dynamic-update-slice_fusion.refs_5_.refs_7_
  76.8 2.7 %collective-permute-start.8 = (bf16[512,2048]{1,0:T(8,128)(2,1)S(1)}, bf16[512,2048]{1,0:T(8,128)(2,1)}, u32[]{:S(2)}, u32[]{:S(2)}) collective-permute-start(bf16[512,2048]{1,0:T(8,128)(2,1)S(1)} %constant_dynamic-update-slice_fusion.refs_5_.refs_7_), channel_id=1, source_target_pairs={{0,32},{32,0},{1,33},{33,1},{2,34},{34,2},{3,35},{35,3},{4,36},{36... | collective-permute-start | bytes 6291464 | tf_op jit(solution)/shard_map/ppermute | solution.py:243
  79.5 0.1 pad_add_fusion.3
  79.6 0.6 pad_add_fusion.1.pos_ref
  80.3 15.2 %all-to-all-done.3.x_ref = bf16[16,32,896]{2,1,0:T(8,128)(2,1)S(1)} async-done(((bf16[16,32,896]{2,1,0:T(8,128)(2,1)}), bf16[16,32,896]{2,1,0:T(8,128)(2,1)S(1)}, u32[]{:S(2)}, u32[]{:S(2)}) %all-to-all-start.3) | async-done | bytes 917536 | tf_op jit(solution)/shard_map/all_to_all | solution.py:275
  95.5 5.2 %all-to-all-start.2 = ((bf16[8,128,128]{2,1,0:T(8,128)(2,1)}), bf16[8,128,128]{2,1,0:T(8,128)(2,1)S(1)}, u32[]{:S(2)}, u32[]{:S(2)}) async-start(bf16[8,128,128]{2,1,0:T(8,128)(2,1)} %self_attention.1), calls=%async_computation.2 | async-start | bytes 524288 | tf_op jit(solution)/shard_map/all_to_all | solution.py:294
  100.6 0.1 add_select_fusion
  100.7 1.9 %choose_rows.1.refs_0_ = bf16[128,896]{1,0:T(8,128)(2,1)} custom-call(s32[1,2,2]{2,1,0:T(2,128)} %own_ref.1, bf16[16,32,896]{2,1,0:T(8,128)(2,1)} %copy-done.1), custom_call_target="tpu_custom_call" | custom-call | tf_op jit(solution)/shard_map/choose_rows/pallas_call | solution.py:108
  102.6 4.2 %collective-permute-start.4 = (bf16[128,896]{1,0:T(8,128)(2,1)}, bf16[128,896]{1,0:T(8,128)(2,1)S(1)}, u32[]{:S(2)}, u32[]{:S(2)}) collective-permute-start(bf16[128,896]{1,0:T(8,128)(2,1)} %choose_rows.1.refs_0_), channel_id=1, source_target_pairs={{0,1},{1,2},{2,3},{3,0},{4,5},{5,6},{6,7},{7,4},{8,9},{9,10},{10,1... | collective-permute-start | bytes 688136 | tf_op jit(solution)/shard_map/ppermute | solution.py:243
  106.8 3.2 %collective-permute-start.5 = (bf16[128,896]{1,0:T(8,128)(2,1)}, bf16[128,896]{1,0:T(8,128)(2,1)S(1)}, u32[]{:S(2)}, u32[]{:S(2)}) collective-permute-start(bf16[128,896]{1,0:T(8,128)(2,1)} %choose_rows.1.refs_0_), channel_id=1, source_target_pairs={{0,3},{1,0},{2,1},{3,2},{4,7},{5,4},{6,5},{7,6},{8,11},{9,8},{10,9... | collective-permute-start | bytes 688136 | tf_op jit(solution)/shard_map/ppermute | solution.py:243
  110.0 6.6 %collective-permute-start.6 = (bf16[128,896]{1,0:T(8,128)(2,1)}, bf16[128,896]{1,0:T(8,128)(2,1)S(1)}, u32[]{:S(2)}, u32[]{:S(2)}) collective-permute-start(bf16[128,896]{1,0:T(8,128)(2,1)} %choose_rows.1.refs_0_), channel_id=1, source_target_pairs={{0,2},{1,3},{2,0},{3,1},{4,6},{5,7},{6,4},{7,5},{8,10},{9,11},{10,... | collective-permute-start | bytes 688136 | tf_op jit(solution)/shard_map/ppermute | solution.py:243
  116.5 1.9 %fusion.refs_4_ = bf16[2,896,512]{2,1,0:T(8,128)(2,1)} fusion(s32[2,512]{1,0:T(2,128)S(1)} %add_select_fusion), kind=kLoop, calls=%fused_computation.1 | loop fusion | flops 1835008 | bytes 1839104 | tf_op jit(solution)/shard_map/convert_element_type | solution.py:309
  118.5 0.0 all-to-all-done.2
  118.5 0.2 copy.12
  118.7 0.9 copy.13
  119.5 0.0 copy-done
  119.5 0.0 collective-permute-done.4.refs_1_
  119.5 2.6 %collective-permute-done.5.refs_2_ = bf16[128,896]{1,0:T(8,128)(2,1)S(1)} collective-permute-done((bf16[128,896]{1,0:T(8,128)(2,1)}, bf16[128,896]{1,0:T(8,128)(2,1)S(1)}, u32[]{:S(2)}, u32[]{:S(2)}) %collective-permute-start.5) | collective-permute-done | bytes 229408 | tf_op jit(solution)/shard_map/ppermute | solution.py:243
  122.1 11.7 %collective-permute-done.6.refs_3_ = bf16[128,896]{1,0:T(8,128)(2,1)S(1)} collective-permute-done((bf16[128,896]{1,0:T(8,128)(2,1)}, bf16[128,896]{1,0:T(8,128)(2,1)S(1)}, u32[]{:S(2)}, u32[]{:S(2)}) %collective-permute-start.6) | collective-permute-done | bytes 229408 | tf_op jit(solution)/shard_map/ppermute | solution.py:243
  133.8 0.0 collective-permute-done.8.refs_6_.refs_8_
  133.9 0.7 copy-done.5
  134.5 8.8 %cross_attention.1 = bf16[1,128,1024]{2,1,0:T(8,128)(2,1)} custom-call(s32[2]{0:T(128)} %pad_add_fusion.1.pos_ref, bf16[128,896]{1,0:T(8,128)(2,1)} %choose_rows.1.refs_0_, bf16[128,896]{1,0:T(8,128)(2,1)} %copy-done.3, bf16[128,896]{1,0:T(8,128)(2,1)} %copy-done.4, bf16[128,896]{1,0:T(8,128)(2,1)} %copy-done.5, bf16[2,896,512]{2,1,0:T(8,128)(2,1)} %fusion.refs_4_, ...), custom_call_target="tpu_custom_call" | custom-call | tf_op jit(solution)/shard_map/cross_attention/pallas_call | solution.py:221
  (17 shorter events, 0.1 us)
Async XLA Ops:
  1.4 3.4 %copy-start.6 = (s32[1,2,4]{2,1,0:T(2,128)}, s32[1,2,4]{2,1,0:T(2,128)S(1)}, u32[]{:S(2)}) copy-start(s32[1,2,4]{2,1,0:T(2,128)S(1)} %pad_add_fusion.own_ref) | copy-start | bytes 100
  1.4 3.4 %collective-permute-start = (s32[1,2,4]{2,1,0:T(2,128)S(1)}, s32[1,2,4]{2,1,0:T(2,128)S(1)}, u32[]{:S(2)}, u32[]{:S(2)}) collective-permute-start(s32[1,2,4]{2,1,0:T(2,128)S(1)} %pad_add_fusion.own_ref), channel_id=1, source_target_pairs={{0,32},{32,0},{1,33},{33,1},{2,34},{34,2},{3,35},{35,3},{4,36},{36... | collective-permute-start | bytes 104 | tf_op jit(solution)/shard_map/ppermute | solution.py:243
  4.8 0.6 copy-start.7
  6.9 21.3 %all-to-all-start = ((bf16[8,8,2048]{2,1,0:T(8,128)(2,1)}), bf16[8,8,2048]{2,1,0:T(8,128)(2,1)S(1)}, u32[]{:S(2)}, u32[]{:S(2)}) async-start(bf16[8,8,2048]{2,1,0:T(8,128)(2,1)} %stage_weights.1), calls=%async_computation | async-start | bytes 524288 | tf_op jit(solution)/shard_map/all_to_all | solution.py:270
  28.1 34.6 %all-to-all-start.1 = ((bf16[8,3,128,128]{3,2,1,0:T(8,128)(2,1)}), bf16[8,3,128,128]{3,2,1,0:T(8,128)(2,1)S(1)}, u32[]{:S(2)}, u32[]{:S(2)}) async-start(bf16[8,3,128,128]{3,2,1,0:T(8,128)(2,1)} %pack_heads.1), calls=%async_computation.1 | async-start | bytes 1572864 | tf_op jit(solution)/shard_map/all_to_all | solution.py:289
  33.3 13.5 %collective-permute-start.1 = (bf16[64,2048]{1,0:T(8,128)(2,1)S(1)}, bf16[64,2048]{1,0:T(8,128)(2,1)S(1)}, u32[]{:S(2)}, u32[]{:S(2)}) collective-permute-start(bf16[64,2048]{1,0:T(8,128)(2,1)S(1)} %bitcast.10), channel_id=1, source_target_pairs={{0,4},{4,0},{1,5},{5,1},{2,6},{6,2},{3,7},{7,3},{8,12},{12,8},{9,1... | collective-permute-start | bytes 786440 | tf_op jit(solution)/shard_map/ppermute | solution.py:243
  46.8 12.8 %collective-permute-start.2 = (bf16[128,2048]{1,0:T(8,128)(2,1)S(1)}, bf16[128,2048]{1,0:T(8,128)(2,1)}, u32[]{:S(2)}, u32[]{:S(2)}) collective-permute-start(bf16[128,2048]{1,0:T(8,128)(2,1)S(1)} %pad_maximum_fusion), channel_id=1, source_target_pairs={{0,8},{8,16},{16,24},{24,0},{1,9},{9,17},{17,25},{25,1},{2,10},{10... | collective-permute-start | bytes 1572872 | tf_op jit(solution)/shard_map/ppermute | solution.py:243
  50.0 23.5 %collective-permute-start.3 = (bf16[128,2048]{1,0:T(8,128)(2,1)S(1)}, bf16[128,2048]{1,0:T(8,128)(2,1)}, u32[]{:S(2)}, u32[]{:S(2)}) collective-permute-start(bf16[128,2048]{1,0:T(8,128)(2,1)S(1)} %pad_maximum_fusion), channel_id=1, source_target_pairs={{0,24},{8,0},{16,8},{24,16},{1,25},{9,1},{17,9},{25,17},{2,26},{10... | collective-permute-start | bytes 1572872 | tf_op jit(solution)/shard_map/ppermute | solution.py:243
  59.6 16.1 %collective-permute-start.7 = (bf16[128,2048]{1,0:T(8,128)(2,1)}, bf16[128,2048]{1,0:T(8,128)(2,1)}, u32[]{:S(2)}, u32[]{:S(2)}) collective-permute-start(bf16[128,2048]{1,0:T(8,128)(2,1)} %collective-permute-done.2), channel_id=1, source_target_pairs={{0,8},{8,16},{16,24},{24,0},{1,9},{9,17},{17,25},{25,1},{2,10},{10... | collective-permute-start | bytes 1572872 | tf_op jit(solution)/shard_map/ppermute | solution.py:243
  62.8 7.3 %copy-start.2 = (bf16[8,3,128,128]{3,2,1,0:T(8,128)(2,1)}, bf16[8,3,128,128]{3,2,1,0:T(8,128)(2,1)S(1)}, u32[]{:S(2)}) copy-start(bf16[8,3,128,128]{3,2,1,0:T(8,128)(2,1)S(1)} %all-to-all-done.1.x_ref) | copy-start | bytes 2359300
  62.8 32.7 %all-to-all-start.3 = ((bf16[16,32,896]{2,1,0:T(8,128)(2,1)}), bf16[16,32,896]{2,1,0:T(8,128)(2,1)S(1)}, u32[]{:S(2)}, u32[]{:S(2)}) async-start(bf16[16,32,896]{2,1,0:T(8,128)(2,1)} %offer_rows.1), calls=%async_computation.3 | async-start | bytes 1835008 | tf_op jit(solution)/shard_map/all_to_all | solution.py:275
  76.8 42.7 %copy-start = (bf16[512,2048]{1,0:T(8,128)(2,1)}, bf16[512,2048]{1,0:T(8,128)(2,1)S(1)}, u32[]{:S(2)}) copy-start(bf16[512,2048]{1,0:T(8,128)(2,1)S(1)} %constant_dynamic-update-slice_fusion.refs_5_.refs_7_) | copy-start | bytes 6291460
  76.8 57.0 %collective-permute-start.8 = (bf16[512,2048]{1,0:T(8,128)(2,1)S(1)}, bf16[512,2048]{1,0:T(8,128)(2,1)}, u32[]{:S(2)}, u32[]{:S(2)}) collective-permute-start(bf16[512,2048]{1,0:T(8,128)(2,1)S(1)} %constant_dynamic-update-slice_fusion.refs_5_.refs_7_), channel_id=1, source_target_pairs={{0,32},{32,0},{1,33},{33,1},{2,34},{34,2},{3,35},{35,3},{4,36},{36... | collective-permute-start | bytes 6291464 | tf_op jit(solution)/shard_map/ppermute | solution.py:243
  95.5 5.2 %copy-start.1 = (bf16[16,32,896]{2,1,0:T(8,128)(2,1)}, bf16[16,32,896]{2,1,0:T(8,128)(2,1)S(1)}, u32[]{:S(2)}) copy-start(bf16[16,32,896]{2,1,0:T(8,128)(2,1)S(1)} %all-to-all-done.3.x_ref) | copy-start | bytes 2752516
  95.5 23.0 %all-to-all-start.2 = ((bf16[8,128,128]{2,1,0:T(8,128)(2,1)}), bf16[8,128,128]{2,1,0:T(8,128)(2,1)S(1)}, u32[]{:S(2)}, u32[]{:S(2)}) async-start(bf16[8,128,128]{2,1,0:T(8,128)(2,1)} %self_attention.1), calls=%async_computation.2 | async-start | bytes 524288 | tf_op jit(solution)/shard_map/all_to_all | solution.py:294
  102.6 16.9 %collective-permute-start.4 = (bf16[128,896]{1,0:T(8,128)(2,1)}, bf16[128,896]{1,0:T(8,128)(2,1)S(1)}, u32[]{:S(2)}, u32[]{:S(2)}) collective-permute-start(bf16[128,896]{1,0:T(8,128)(2,1)} %choose_rows.1.refs_0_), channel_id=1, source_target_pairs={{0,1},{1,2},{2,3},{3,0},{4,5},{5,6},{6,7},{7,4},{8,9},{9,10},{10,1... | collective-permute-start | bytes 688136 | tf_op jit(solution)/shard_map/ppermute | solution.py:243
  106.8 15.3 %collective-permute-start.5 = (bf16[128,896]{1,0:T(8,128)(2,1)}, bf16[128,896]{1,0:T(8,128)(2,1)S(1)}, u32[]{:S(2)}, u32[]{:S(2)}) collective-permute-start(bf16[128,896]{1,0:T(8,128)(2,1)} %choose_rows.1.refs_0_), channel_id=1, source_target_pairs={{0,3},{1,0},{2,1},{3,2},{4,7},{5,4},{6,5},{7,6},{8,11},{9,8},{10,9... | collective-permute-start | bytes 688136 | tf_op jit(solution)/shard_map/ppermute | solution.py:243
  110.0 23.9 %collective-permute-start.6 = (bf16[128,896]{1,0:T(8,128)(2,1)}, bf16[128,896]{1,0:T(8,128)(2,1)S(1)}, u32[]{:S(2)}, u32[]{:S(2)}) collective-permute-start(bf16[128,896]{1,0:T(8,128)(2,1)} %choose_rows.1.refs_0_), channel_id=1, source_target_pairs={{0,2},{1,3},{2,0},{3,1},{4,6},{5,7},{6,4},{7,5},{8,10},{9,11},{10,... | collective-permute-start | bytes 688136 | tf_op jit(solution)/shard_map/ppermute | solution.py:243
  119.5 14.3 %copy-start.3 = (bf16[128,896]{1,0:T(8,128)(2,1)}, bf16[128,896]{1,0:T(8,128)(2,1)S(1)}, u32[]{:S(2)}) copy-start(bf16[128,896]{1,0:T(8,128)(2,1)S(1)} %collective-permute-done.4.refs_1_) | copy-start | bytes 688132
  122.1 11.7 %copy-start.4 = (bf16[128,896]{1,0:T(8,128)(2,1)}, bf16[128,896]{1,0:T(8,128)(2,1)S(1)}, u32[]{:S(2)}) copy-start(bf16[128,896]{1,0:T(8,128)(2,1)S(1)} %collective-permute-done.5.refs_2_) | copy-start | bytes 688132
  133.8 0.7 copy-start.5
